TPU v7x, 512 devices: a whole 4x4x16 slice. The times are simulated.
512 devices in a mesh: ctx: 32 (over z_hi, y, x), head: 16 (over z_lo, core).
Axes of the slice: x: 4, y: 4, z: 16 (z_hi: 2, z_lo: 8; z = z_hi * 8 + z_lo), core: 2. Of those that a mesh axis runs over, the one named last changes fastest.
Arguments:
- stream: bfloat16 [8192, 8192], P('ctx', 'head')
- norm_gain: float32 [8192], replicated, may hold values from 0.1 to 1.9
- tile_vals: bfloat16 [16, 96, 128, 128], P('head', 'ctx')
- tile_row: int32 [16, 96], P('head'), may hold values from 0 to 63, as said below
- tile_col: int32 [16, 96], P('head'), may hold values from 0 to 5, as said below
- kept_count: int32 [16], P('head'), may hold values from 32 to 96, as said below
Outputs:
- attended: bfloat16 [8192, 4096], P('ctx', 'head')
Inputs may be any that keep to these rules, and one draw needn't show every extreme that they name: `tile_row`: for each reader, its first kept_count slots name distinct (row block, column block) pairs; the other slots are unused. For every head of a reader, some row block holds both that head's query tile and its key tile among the live slots. `tile_col`: column block within the reader's 6 blocks. `kept_count`: some reader has all 96 slots live.
All inputs are finite; a program needn't handle non-finite values.
Results may differ from a plain program's by a relative error of at most 0.04.
Values may be sent and summed in bfloat16 or wider, within the bound.
No kernel may reach another device: no remote copies, remote signals or barrier semaphores. Data moves between devices by JAX's collectives and lax.ppermute only.
A program may use at most 64 MiB of HBM per device.

v0:
```python
import functools
import math

import jax
import jax.numpy as jnp
from jax import lax
from jax.experimental import pallas as pl
from jax.experimental.pallas import tpu as pltpu
from jax.sharding import Mesh
from jax.sharding import PartitionSpec as P

D = 8192
HD = 128
TOK = 256
ROWS = D // HD
COLS = 6
PLANE = ("y", "x")
CTX = ("zh",) + PLANE
HEAD = ("zl", "core")
NEG = -1e30

rope_base = 1000000.0


VM = pl.BlockSpec(memory_space=pltpu.VMEM)
SM = pl.BlockSpec(memory_space=pltpu.SMEM)


def params(mib):
    return pltpu.CompilerParams(vmem_limit_bytes=mib * 1024 * 1024)


def scatter_kernel(row_ref, col_ref, live_ref, near_ref, there_ref, w_ref):
    def clear(i, c):
        w_ref[i] = jnp.zeros((HD, COLS * HD), jnp.bfloat16)
        return c

    lax.fori_loop(0, ROWS, clear, 0)
    half = near_ref.shape[0]
    for n, ref in enumerate((near_ref, there_ref)):

        def put(s, c, n=n, ref=ref):
            slot = n * half + s

            @pl.when(live_ref[slot] > 0)
            def _():
                at = pl.multiple_of(col_ref[slot] * HD, HD)
                w_ref[row_ref[slot], :, pl.ds(at, HD)] = ref[s]

            return c

        lax.fori_loop(0, half, put, 0)


def scatter(rows, cols, live, near_tiles, there_tiles):
    return pl.pallas_call(
        scatter_kernel,
        out_shape=jax.ShapeDtypeStruct((ROWS, HD, COLS * HD), jnp.bfloat16),
        in_specs=[SM, SM, SM, VM, VM],
        out_specs=VM,
        compiler_params=params(4),
        name="scatter_tiles",
    )(rows, cols, live, near_tiles, there_tiles)


def project_kernel(core_ref, mine_ref, other_ref, w_ref, gain_ref, cos_ref, sin_ref,
                   q_ref, kv_ref, acc_ref):
    core = core_ref[0]
    chunk = mine_ref.shape[2]
    per = chunk // HD

    def square(i, tot):
        for ref in (mine_ref, other_ref):
            for k in range(per):
                v = ref[i, :, k * HD:(k + 1) * HD].astype(jnp.float32)
                tot = tot + v * v
        return tot

    tot = lax.fori_loop(0, 8, square, jnp.zeros((TOK, HD), jnp.float32))
    r = lax.rsqrt(jnp.sum(tot, axis=1, keepdims=True) / D + 1e-05)
    acc_ref[...] = jnp.zeros_like(acc_ref)

    def step(i, c):
        part = None
        for ref, cc in ((mine_ref, core), (other_ref, 1 - core)):
            x = ref[i].astype(jnp.float32) * r * gain_ref[2 * i + cc]
            w = w_ref[pl.ds((2 * i + cc) * per, per)].reshape(chunk, COLS * HD)
            d = jnp.dot(x.astype(jnp.bfloat16), w, preferred_element_type=jnp.float32)
            part = d if part is None else part + d
        acc_ref[...] += part
        return c

    lax.fori_loop(0, 8, step, 0)
    cosines = cos_ref[...]
    sines = sin_ref[...]

    def rot(v):
        return v * cosines + pltpu.roll(v, HD // 2, 1) * sines

    for h in range(2):
        q = rot(acc_ref[:, h * HD:(h + 1) * HD])
        k = rot(acc_ref[:, (2 + h) * HD:(3 + h) * HD]).astype(jnp.bfloat16)
        v = acc_ref[:, (4 + h) * HD:(5 + h) * HD]
        for half in range(2):
            at = slice(half * HD, (half + 1) * HD)
            qt = q[at].T.astype(jnp.bfloat16)
            for copy in range(4):
                q_ref[copy, 2 * h + half] = qt
            kv_ref[4 * h + half] = k[at]
            kv_ref[4 * h + 2 + half] = v[at].T.astype(jnp.bfloat16)


def project(core, mine, other, w, gain, cosines, sines):
    return pl.pallas_call(
        project_kernel,
        out_shape=(
            jax.ShapeDtypeStruct((4, 4, HD, HD), jnp.bfloat16),
            jax.ShapeDtypeStruct((8, HD, HD), jnp.bfloat16),
        ),
        in_specs=[SM] + [VM] * 6,
        out_specs=(VM, VM),
        scratch_shapes=[pltpu.VMEM((TOK, COLS * HD), jnp.float32)],
        compiler_params=params(10),
        name="project",
    )(core, mine, other, w, gain, cosines, sines)


SCALE = math.log2(math.e) / math.sqrt(HD)


def load_q(q_ref, n, h):
    return jnp.concatenate([q_ref[n, 2 * h], q_ref[n, 2 * h + 1]], axis=1)


def load_k(ref, h):
    return ref[2 * h * 2:2 * h * 2 + 2].reshape(TOK, HD)


def load_v(ref, h):
    return jnp.concatenate([ref[4 * h + 2], ref[4 * h + 3]], axis=1)


def near_kernel(ids_ref, q_ref, k0_ref, k1_ref, k2_ref, k3_ref, acc_ref, stat_ref):
    y = ids_ref[1]
    x = ids_ref[2]
    refs = (k0_ref, k1_ref, k2_ref, k3_ref)
    kids = [4 * lax.rem(y + 4 - k, 4) + x for k in range(4)]
    gap = lax.broadcasted_iota(jnp.int32, (TOK, TOK), 0) - lax.broadcasted_iota(
        jnp.int32, (TOK, TOK), 1
    )

    def one_source(n, c):
        qid = 4 * y + n
        for h in range(2):
            q = load_q(q_ref, n, h)
            ss = []
            for ref, kid in zip(refs, kids):
                s = jnp.dot(load_k(ref, h), q, preferred_element_type=jnp.float32)
                ss.append(jnp.where(gap <= (qid - kid) * TOK, s, NEG))
            top = functools.reduce(jnp.maximum, [jnp.max(s, axis=0, keepdims=True) for s in ss])
            acc = None
            total = None
            for ref, kid, s in zip(refs, kids, ss):
                p = jnp.where(gap <= (qid - kid) * TOK, jnp.exp2((s - top) * SCALE), 0.0)
                t = jnp.sum(p, axis=0, keepdims=True)
                o = jnp.dot(
                    load_v(ref, h), p.astype(jnp.bfloat16), preferred_element_type=jnp.float32
                )
                acc = o if acc is None else acc + o
                total = t if total is None else total + t
            acc_ref[2 * n + h] = acc
            stat_ref[2 * n + h, 0:1] = top
            stat_ref[2 * n + h, 1:2] = total
        return c

    lax.fori_loop(0, 4, one_source, 0)


STATE = (
    jax.ShapeDtypeStruct((8, HD, TOK), jnp.float32),
    jax.ShapeDtypeStruct((8, 8, TOK), jnp.float32),
)


def near(ids, q, keys):
    return pl.pallas_call(
        near_kernel,
        out_shape=STATE,
        in_specs=[SM] + [VM] * 5,
        out_specs=(VM, VM),
        compiler_params=params(10),
        name="attend_near",
    )(ids, q, *keys)


def fold(q_ref, refs, n, h, acc, old, total):
    q = load_q(q_ref, n, h)
    ss = [jnp.dot(load_k(ref, h), q, preferred_element_type=jnp.float32) for ref in refs]
    top = functools.reduce(jnp.maximum, [jnp.max(s, axis=0, keepdims=True) for s in ss], old)
    fac = jnp.exp2((old - top) * SCALE)
    acc = acc * fac
    total = total * fac
    for s, ref in zip(ss, refs):
        p = jnp.exp2((s - top) * SCALE)
        total = total + jnp.sum(p, axis=0, keepdims=True)
        acc = acc + jnp.dot(
            load_v(ref, h), p.astype(jnp.bfloat16), preferred_element_type=jnp.float32
        )
    return acc, top, total


def far_kernel(ids_ref, q_ref, k0_ref, k1_ref, acc_in, stat_in, acc_ref, stat_ref):
    late = ids_ref[0] > 0

    def one_source(n, c):
        for h in range(2):
            i = 2 * n + h
            acc = acc_in[i]
            top = stat_in[i, 0:1]
            total = stat_in[i, 1:2]
            acc, top, total = fold(q_ref, (k0_ref, k1_ref), n, h, acc, top, total)
            acc_ref[i] = acc
            stat_ref[i, 0:1] = top
            stat_ref[i, 1:2] = total
        return c

    @pl.when(late)
    def _():
        lax.fori_loop(0, 4, one_source, 0)

    @pl.when(jnp.logical_not(late))
    def _():
        acc_ref[...] = acc_in[...]
        stat_ref[...] = stat_in[...]


def far(ids, q, fars, acc, stat):
    return pl.pallas_call(
        far_kernel,
        out_shape=STATE,
        in_specs=[SM] + [VM] * 5,
        out_specs=(VM, VM),
        compiler_params=params(10),
        name="attend_far",
    )(ids, q, *fars, acc, stat)


def last_kernel(ids_ref, q_ref, k0_ref, k1_ref, acc_ref, stat_ref, out_ref):
    late = ids_ref[0] > 0

    def finish(n, h, acc, top, total):
        some = total > 0
        safe = jnp.where(some, total, 1.0)
        lse = jnp.where(some, top * SCALE + jnp.log2(safe), NEG)
        at = slice(h * TOK, (h + 1) * TOK)
        out_ref[n, 0:HD, at] = (acc / safe).astype(jnp.bfloat16)
        hi = lse.astype(jnp.bfloat16).astype(jnp.float32)
        mid = (lse - hi).astype(jnp.bfloat16).astype(jnp.float32)
        low = lse - hi - mid
        r = lax.broadcasted_iota(jnp.int32, (16, TOK), 0)
        extra = jnp.where(r == 0, hi, jnp.where(r == 1, mid, jnp.where(r == 2, low, 0.0)))
        out_ref[n, HD:HD + 16, at] = extra.astype(jnp.bfloat16)

    def state(n, h):
        i = 2 * n + h
        return acc_ref[i], stat_ref[i, 0:1], stat_ref[i, 1:2]

    @pl.when(jnp.logical_not(late))
    def _():
        def one_source(n, c):
            for h in range(2):
                finish(n, h, *state(n, h))
            return c

        lax.fori_loop(0, 4, one_source, 0)

    @pl.when(late)
    def _():
        def one_source(n, c):
            for h in range(2):
                finish(n, h, *fold(q_ref, (k0_ref, k1_ref), n, h, *state(n, h)))
            return c

        lax.fori_loop(0, 4, one_source, 0)


def last(ids, q, fars, acc, stat):
    return pl.pallas_call(
        last_kernel,
        out_shape=jax.ShapeDtypeStruct((4, HD + 16, 2 * TOK), jnp.bfloat16),
        in_specs=[SM] + [VM] * 5,
        out_specs=VM,
        compiler_params=params(10),
        name="attend_last",
    )(ids, q, *fars, acc, stat)


def combine_kernel(parts_ref, out_ref):
    count = parts_ref.shape[0]
    lses = []
    for i in range(count):
        e = parts_ref[i, HD:HD + 16].astype(jnp.float32)
        lses.append(e[0:1] + e[1:2] + e[2:3])
    top = functools.reduce(jnp.maximum, lses)
    ws = [jnp.exp2(v - top) for v in lses]
    tot = sum(ws)
    o = None
    for i in range(count):
        t = parts_ref[i, 0:HD].astype(jnp.float32) * (ws[i] / tot)
        o = t if o is None else o + t
    out_ref[:, :HD] = o[:, :TOK].T.astype(jnp.bfloat16)
    out_ref[:, HD:] = o[:, TOK:].T.astype(jnp.bfloat16)


def combine(parts):
    return pl.pallas_call(
        combine_kernel,
        out_shape=jax.ShapeDtypeStruct((TOK, 2 * HD), jnp.bfloat16),
        in_specs=[VM],
        out_specs=VM,
        compiler_params=params(10),
        name="combine",
    )(parts)


def spread(x, axis, n):
    many = jnp.broadcast_to(x[None], (n,) + x.shape)
    return lax.all_to_all(many, axis, 0, 0, tiled=True)


def body(stream, norm_gain, tile_vals, tile_row, tile_col, kept_count):
    zh = lax.axis_index("zh")
    core = lax.axis_index("core")
    plane = lax.axis_index(PLANE)
    block = zh * 16 + plane
    mine = lax.all_gather(stream, "zl", axis=0, tiled=False)
    tv = tile_vals[0]
    there = lax.ppermute(tv, "zh", [(0, 1), (1, 0)])
    near_tiles = spread(tv, PLANE, 16).reshape(-1, HD, HD)
    there_tiles = spread(there, PLANE, 16).reshape(-1, HD, HD)

    def order(v):
        v = v.reshape(2, 48)
        return jnp.where(zh == 0, v, v[::-1]).reshape(96)

    rows = order(tile_row[0])
    cols = order(tile_col[0])
    slot = order(jnp.arange(96, dtype=jnp.int32))
    live = (slot < kept_count[0]).astype(jnp.int32)
    half = HD // 2
    freq = jnp.exp(-math.log(rope_base) * jnp.arange(half, dtype=jnp.float32) / half)
    qpos = block * TOK + jnp.arange(TOK, dtype=jnp.int32)
    angles = qpos.astype(jnp.float32)[:, None] * freq[None, :]
    c = jnp.cos(angles)
    s = jnp.sin(angles)
    cosines = jnp.concatenate([c, c], axis=1)
    sines = jnp.concatenate([-s, s], axis=1)
    gain = norm_gain.reshape(16, 1, 512)
    mine, near_tiles, there_tiles, rows, cols, live, gain, cosines, sines = (
        lax.optimization_barrier(
            (mine, near_tiles, there_tiles, rows, cols, live, gain, cosines, sines)
        )
    )
    other = lax.ppermute(mine, "core", [(0, 1), (1, 0)])
    w = scatter(rows, cols, live, near_tiles, there_tiles)
    q, kv = project(core.reshape(1), mine, other, w, gain, cosines, sines)
    fars = []
    for k in range(4):
        pairs = [
            (4 * y + x, 16 + 4 * ((y + k) % 4) + x) for y in range(4) for x in range(4)
        ]
        fars.append(lax.ppermute(kv, CTX, pairs))
    keys = [kv]
    for k in range(1, 4):
        keys.append(lax.ppermute(kv, "y", [(y, y + k) for y in range(4 - k)]))
    q = lax.all_to_all(q, "x", 0, 0, tiled=True)
    ids = jnp.stack([zh, lax.axis_index("y"), lax.axis_index("x")]).astype(jnp.int32)
    acc, stat = near(ids, q, keys)
    acc, stat = far(ids, q, fars[:2], acc, stat)
    parts = lax.all_to_all(last(ids, q, fars[2:], acc, stat), "x", 0, 0, tiled=True)
    return combine(parts)


def solution(mesh):
    wide = Mesh(mesh.devices.reshape(2, 4, 4, 8, 2), CTX + HEAD)
    return jax.shard_map(
        body,
        mesh=wide,
        in_specs=(
            P(CTX, HEAD),
            P(),
            P(HEAD, CTX, None, None),
            P(HEAD, None),
            P(HEAD, None),
            P(HEAD),
        ),
        out_specs=P(CTX, HEAD),
        check_vma=False,
    )
```

profile of v0, /device:TPU:472, one launch (start us, length us, event | category | flops | bytes accessed | tf_op | source)
XLA Modules:
  0.0 230.8 jit_solution(6759310090150522569)
XLA Ops:
  7.3 2.4 %broadcast_in_dim.7 = bf16[16,3,128,128]{3,2,1,0:T(8,128)(2,1)} broadcast(bf16[3,128,128]{2,1,0:T(8,128)(2,1)} %bitcast.16), dimensions={1,2,3} | broadcast | bytes 1671168 | tf_op jit(solution)/shard_map/broadcast_in_dim | solution.py:327
  9.7 7.3 %all-to-all-start = ((bf16[16,3,128,128]{3,2,1,0:T(8,128)(2,1)}), bf16[16,3,128,128]{3,2,1,0:T(8,128)(2,1)S(1)}, u32[]{:S(2)}, u32[]{:S(2)}) async-start(bf16[16,3,128,128]{3,2,1,0:T(8,128)(2,1)} %broadcast_in_dim.7), calls=%async_computation | async-start | bytes 3145728 | tf_op jit(solution)/shard_map/all_to_all | solution.py:328
  17.0 5.4 %collective-permute-start = (bf16[3,128,128]{2,1,0:T(8,128)(2,1)S(1)}, bf16[3,128,128]{2,1,0:T(8,128)(2,1)S(1)}, u32[]{:S(2)}, u32[]{:S(2)}) collective-permute-start(bf16[3,128,128]{2,1,0:T(8,128)(2,1)S(1)} %bitcast.17), channel_id=1, source_target_pairs={{0,256},{256,0},{1,257},{257,1},{2,258},{258,2},{3,259},{259,3},{4... | collective-permute-start | bytes 294920 | tf_op jit(solution)/shard_map/ppermute | solution.py:338
  22.4 16.2 %collective-permute-done = bf16[3,128,128]{2,1,0:T(8,128)(2,1)S(1)} collective-permute-done((bf16[3,128,128]{2,1,0:T(8,128)(2,1)S(1)}, bf16[3,128,128]{2,1,0:T(8,128)(2,1)S(1)}, u32[]{:S(2)}, u32[]{:S(2)}) %collective-permute-start) | collective-permute-done | bytes 98336 | tf_op jit(solution)/shard_map/ppermute | solution.py:338
  38.6 0.9 all-to-all-done
  39.5 1.5 broadcast_in_dim.8
  41.0 6.5 %all-to-all-start.1 = ((bf16[16,3,128,128]{3,2,1,0:T(8,128)(2,1)}), bf16[16,3,128,128]{3,2,1,0:T(8,128)(2,1)S(1)}, u32[]{:S(2)}, u32[]{:S(2)}) async-start(bf16[16,3,128,128]{3,2,1,0:T(8,128)(2,1)} %broadcast_in_dim.8), calls=%async_computation.1 | async-start | bytes 3145728 | tf_op jit(solution)/shard_map/all_to_all | solution.py:328
  51.3 15.8 %all-to-all-done.1 = bf16[16,3,128,128]{3,2,1,0:T(8,128)(2,1)S(1)} async-done(((bf16[16,3,128,128]{3,2,1,0:T(8,128)(2,1)}), bf16[16,3,128,128]{3,2,1,0:T(8,128)(2,1)S(1)}, u32[]{:S(2)}, u32[]{:S(2)}) %all-to-all-start.1) | async-done | bytes 1572896 | tf_op jit(solution)/shard_map/all_to_all | solution.py:328
  67.1 10.5 %all-gather.3.cloned.1.call-done = bf16[2048,512]{1,0:T(8,128)(2,1)} async-done(((bf16[256,512]{1,0:T(8,128)(2,1)}), bf16[2048,512]{1,0:T(8,128)(2,1)}) %all-gather.3.cloned.1.call-update) | async-done | bytes 2097168 | tf_op jit(solution)/shard_map/all_gather | solution.py:336
  77.6 1.9 collective-permute-start.1
  79.5 3.1 %scatter_tiles.1.w_ref = bf16[64,128,768]{2,1,0:T(8,128)(2,1)S(1)} custom-call(s32[96]{0:T(128)S(1)} %reshape.48.row_ref, s32[96]{0:T(128)S(1)} %reshape.49.col_ref, s32[96]{0:T(128)S(1)} %reshape.54.live_ref, bf16[48,128,128]{2,1,0:T(8,128)(2,1)S(1)} %bitcast.11, bf16[48,128,128]{2,1,0:T(8,128)(2,1)S(1)} %bitcast.12), custom_call_target="tpu_custom_call" | custom-call | tf_op jit(solution)/shard_map/scatter_tiles/pallas_call | solution.py:56
  82.6 1.3 collective-permute-done.1.other_ref
  84.0 8.6 %project.1 = (bf16[4,4,128,128]{3,2,1,0:T(8,128)(2,1)}, bf16[8,128,128]{2,1,0:T(8,128)(2,1)S(1)}) custom-call(s32[1]{0:T(128)} %bitcast.3.core_ref, bf16[8,256,512]{2,1,0:T(8,128)(2,1)S(1)} %bitcast.14, bf16[8,256,512]{2,1,0:T(8,128)(2,1)} %collective-permute-done.1.other_ref, bf16[64,128,768]{2,1,0:T(8,128)(2,1)S(1)} %scatter_tiles.1.w_ref, ...), custom_call_target="tpu_custom_call" | custom-call | tf_op jit(solution)/shard_map/project/pallas_call | solution.py:114
  92.6 1.3 collective-permute-start.6
  93.9 1.3 collective-permute-start.7
  95.2 4.3 %all-to-all-start.2 = ((bf16[4,4,128,128]{3,2,1,0:T(8,128)(2,1)}), bf16[4,4,128,128]{3,2,1,0:T(8,128)(2,1)S(1)}, u32[]{:S(2)}, u32[]{:S(2)}) async-start(bf16[4,4,128,128]{3,2,1,0:T(8,128)(2,1)} %get-tuple-element.29), calls=%async_computation.2 | async-start | bytes 1048576 | tf_op jit(solution)/shard_map/all_to_all | solution.py:376
  99.5 1.3 collective-permute-start.8
  100.8 1.3 collective-permute-start.4
  102.1 1.3 collective-permute-start.5
  103.4 1.3 collective-permute-start.2
  104.7 0.9 collective-permute-done.7.k2_ref
  105.6 1.3 collective-permute-start.3
  107.0 5.5 %collective-permute-done.8.k3_ref = bf16[8,128,128]{2,1,0:T(8,128)(2,1)S(1)} collective-permute-done((bf16[8,128,128]{2,1,0:T(8,128)(2,1)S(1)}, bf16[8,128,128]{2,1,0:T(8,128)(2,1)S(1)}, u32[]{:S(2)}, u32[]{:S(2)}) %collective-permute-start.8) | collective-permute-done | bytes 262176 | tf_op jit(solution)/shard_map/ppermute | solution.py:375
  112.5 6.5 %attend_near.1 = (f32[8,128,256]{2,1,0:T(8,128)S(1)}, f32[8,8,256]{2,1,0:T(8,128)S(1)}) custom-call(s32[3]{0:T(128)S(1)} %pad_add_fusion.ids_ref, bf16[4,4,128,128]{3,2,1,0:T(8,128)(2,1)S(1)} %all-to-all-done.2.q_ref, bf16[8,128,128]{2,1,0:T(8,128)(2,1)S(1)} %get-tuple-element.30.k0_ref, bf16[8,128,128]{2,1,0:T(8,128)(2,1)S(1)} %collective-permute-done.6.k1_ref, ...), custom_call_target="tpu_custom_call" | custom-call | tf_op jit(solution)/shard_map/attend_near/pallas_call | solution.py:186
  119.0 63.8 %collective-permute-done.4.k0_ref = bf16[8,128,128]{2,1,0:T(8,128)(2,1)S(1)} collective-permute-done((bf16[8,128,128]{2,1,0:T(8,128)(2,1)S(1)}, bf16[8,128,128]{2,1,0:T(8,128)(2,1)S(1)}, u32[]{:S(2)}, u32[]{:S(2)}) %collective-permute-start.4) | collective-permute-done | bytes 262176 | tf_op jit(solution)/shard_map/ppermute | solution.py:372
  182.8 6.9 %collective-permute-done.5.k1_ref = bf16[8,128,128]{2,1,0:T(8,128)(2,1)S(1)} collective-permute-done((bf16[8,128,128]{2,1,0:T(8,128)(2,1)S(1)}, bf16[8,128,128]{2,1,0:T(8,128)(2,1)S(1)}, u32[]{:S(2)}, u32[]{:S(2)}) %collective-permute-start.5) | collective-permute-done | bytes 262176 | tf_op jit(solution)/shard_map/ppermute | solution.py:372
  189.7 4.0 %attend_far.1 = (f32[8,128,256]{2,1,0:T(8,128)S(1)}, f32[8,8,256]{2,1,0:T(8,128)S(1)}) custom-call(s32[3]{0:T(128)S(1)} %pad_add_fusion.ids_ref, bf16[4,4,128,128]{3,2,1,0:T(8,128)(2,1)S(1)} %all-to-all-done.2.q_ref, bf16[8,128,128]{2,1,0:T(8,128)(2,1)S(1)} %collective-permute-done.4.k0_ref, bf16[8,128,128]{2,1,0:T(8,128)(2,1)S(1)} %collective-permute-done.5.k1_ref, ...), custom_call_target="tpu_custom_call" | custom-call | tf_op jit(solution)/shard_map/attend_far/pallas_call | solution.py:238
  193.7 3.0 %collective-permute-done.2.k0_ref = bf16[8,128,128]{2,1,0:T(8,128)(2,1)S(1)} collective-permute-done((bf16[8,128,128]{2,1,0:T(8,128)(2,1)S(1)}, bf16[8,128,128]{2,1,0:T(8,128)(2,1)S(1)}, u32[]{:S(2)}, u32[]{:S(2)}) %collective-permute-start.2) | collective-permute-done | bytes 262176 | tf_op jit(solution)/shard_map/ppermute | solution.py:372
  196.8 7.7 %collective-permute-done.3.k1_ref = bf16[8,128,128]{2,1,0:T(8,128)(2,1)S(1)} collective-permute-done((bf16[8,128,128]{2,1,0:T(8,128)(2,1)S(1)}, bf16[8,128,128]{2,1,0:T(8,128)(2,1)S(1)}, u32[]{:S(2)}, u32[]{:S(2)}) %collective-permute-start.3) | collective-permute-done | bytes 262176 | tf_op jit(solution)/shard_map/ppermute | solution.py:372
  204.4 4.1 %attend_last.1 = bf16[4,144,512]{2,1,0:T(8,128)(2,1)S(1)} custom-call(s32[3]{0:T(128)S(1)} %pad_add_fusion.ids_ref, bf16[4,4,128,128]{3,2,1,0:T(8,128)(2,1)S(1)} %all-to-all-done.2.q_ref, bf16[8,128,128]{2,1,0:T(8,128)(2,1)S(1)} %collective-permute-done.2.k0_ref, bf16[8,128,128]{2,1,0:T(8,128)(2,1)S(1)} %collective-permute-done.3.k1_ref, ...), custom_call_target="tpu_custom_call" | custom-call | tf_op jit(solution)/shard_map/attend_last/pallas_call | solution.py:288
  208.5 14.6 %all_to_all.20.parts_ref = bf16[4,144,512]{2,1,0:T(8,128)(2,1)S(1)} all-to-all(bf16[4,144,512]{2,1,0:T(8,128)(2,1)S(1)} %attend_last.1), channel_id=1, replica_groups=mesh['zh'=2,'y'=4,'x'=4,'zl'=8,'core'=2] {'x'}, dimensions={0} | all-to-all | bytes 1179648 | tf_op jit(solution)/shard_map/all_to_all | solution.py:380
  223.1 0.9 combine.1
  (33 shorter events, 3.9 us)
Async XLA Ops:
  6.5 71.0 %all-gather.3.cloned.1.call-start = ((), (), s32[]{:S(2)}) async-start(), calls=%async_computation.4 | async-start | bytes 2359296 | tf_op jit(solution)/shard_map/all_gather | solution.py:336
  9.7 7.3 %copy-start.2 = (bf16[1,3,128,128]{3,2,1,0:T(8,128)(2,1)S(1)}, bf16[1,3,128,128]{3,2,1,0:T(8,128)(2,1)}, u32[]{:S(2)}) copy-start(bf16[1,3,128,128]{3,2,1,0:T(8,128)(2,1)} %param.8) | copy-start | bytes 294916
  9.7 29.8 %all-to-all-start = ((bf16[16,3,128,128]{3,2,1,0:T(8,128)(2,1)}), bf16[16,3,128,128]{3,2,1,0:T(8,128)(2,1)S(1)}, u32[]{:S(2)}, u32[]{:S(2)}) async-start(bf16[16,3,128,128]{3,2,1,0:T(8,128)(2,1)} %broadcast_in_dim.7), calls=%async_computation | async-start | bytes 3145728 | tf_op jit(solution)/shard_map/all_to_all | solution.py:328
  17.0 21.6 %collective-permute-start = (bf16[3,128,128]{2,1,0:T(8,128)(2,1)S(1)}, bf16[3,128,128]{2,1,0:T(8,128)(2,1)S(1)}, u32[]{:S(2)}, u32[]{:S(2)}) collective-permute-start(bf16[3,128,128]{2,1,0:T(8,128)(2,1)S(1)} %bitcast.17), channel_id=1, source_target_pairs={{0,256},{256,0},{1,257},{257,1},{2,258},{258,2},{3,259},{259,3},{4... | collective-permute-start | bytes 294920 | tf_op jit(solution)/shard_map/ppermute | solution.py:338
  41.0 7.1 %copy-start.3 = (s32[1,96]{1,0:T(1,128)S(1)}, s32[1,96]{1,0:T(1,128)}, u32[]{:S(2)}) copy-start(s32[1,96]{1,0:T(1,128)} %param.10) | copy-start | bytes 1156
  41.0 7.8 %copy-start.4 = (s32[1,96]{1,0:T(1,128)S(1)}, s32[1,96]{1,0:T(1,128)}, u32[]{:S(2)}) copy-start(s32[1,96]{1,0:T(1,128)} %param.9) | copy-start | bytes 1156
  41.0 26.0 %all-to-all-start.1 = ((bf16[16,3,128,128]{3,2,1,0:T(8,128)(2,1)}), bf16[16,3,128,128]{3,2,1,0:T(8,128)(2,1)S(1)}, u32[]{:S(2)}, u32[]{:S(2)}) async-start(bf16[16,3,128,128]{3,2,1,0:T(8,128)(2,1)} %broadcast_in_dim.8), calls=%async_computation.1 | async-start | bytes 3145728 | tf_op jit(solution)/shard_map/all_to_all | solution.py:328
  77.6 6.4 %collective-permute-start.1 = (bf16[8,256,512]{2,1,0:T(8,128)(2,1)}, bf16[8,256,512]{2,1,0:T(8,128)(2,1)}, u32[]{:S(2)}, u32[]{:S(2)}) collective-permute-start(bf16[8,256,512]{2,1,0:T(8,128)(2,1)} %bitcast.13), channel_id=1, source_target_pairs={{0,1},{1,0},{2,3},{3,2},{4,5},{5,4},{6,7},{7,6},{8,9},{9,8},{10,11... | collective-permute-start | bytes 6291464 | tf_op jit(solution)/shard_map/ppermute | solution.py:364
  79.5 4.5 %copy-start = (bf16[2048,512]{1,0:T(8,128)(2,1)S(1)}, bf16[2048,512]{1,0:T(8,128)(2,1)}, u32[]{:S(2)}) copy-start(bf16[2048,512]{1,0:T(8,128)(2,1)} %all-gather.3.cloned.1.call-done) | copy-start | bytes 6291460
  79.5 4.5 %copy-start.1 = (f32[8192]{0:T(1024)S(1)}, f32[8192]{0:T(1024)}, u32[]{:S(2)}) copy-start(f32[8192]{0:T(1024)} %param.7) | copy-start | bytes 98308
  92.6 10.8 %collective-permute-start.6 = (bf16[8,128,128]{2,1,0:T(8,128)(2,1)S(1)}, bf16[8,128,128]{2,1,0:T(8,128)(2,1)S(1)}, u32[]{:S(2)}, u32[]{:S(2)}) collective-permute-start(bf16[8,128,128]{2,1,0:T(8,128)(2,1)S(1)} %get-tuple-element.30.k0_ref), channel_id=1, source_target_pairs={{0,64},{64,128},{128,192},{1,65},{65,129},{129,193},{2,66},{66,130... | collective-permute-start | bytes 786440 | tf_op jit(solution)/shard_map/ppermute | solution.py:375
  93.9 11.7 %collective-permute-start.7 = (bf16[8,128,128]{2,1,0:T(8,128)(2,1)S(1)}, bf16[8,128,128]{2,1,0:T(8,128)(2,1)S(1)}, u32[]{:S(2)}, u32[]{:S(2)}) collective-permute-start(bf16[8,128,128]{2,1,0:T(8,128)(2,1)S(1)} %get-tuple-element.30.k0_ref), channel_id=1, source_target_pairs={{0,128},{64,192},{1,129},{65,193},{2,130},{66,194},{3,131},{67,195... | collective-permute-start | bytes 786440 | tf_op jit(solution)/shard_map/ppermute | solution.py:375
  95.2 17.3 %all-to-all-start.2 = ((bf16[4,4,128,128]{3,2,1,0:T(8,128)(2,1)}), bf16[4,4,128,128]{3,2,1,0:T(8,128)(2,1)S(1)}, u32[]{:S(2)}, u32[]{:S(2)}) async-start(bf16[4,4,128,128]{3,2,1,0:T(8,128)(2,1)} %get-tuple-element.29), calls=%async_computation.2 | async-start | bytes 1048576 | tf_op jit(solution)/shard_map/all_to_all | solution.py:376
  99.5 13.0 %collective-permute-start.8 = (bf16[8,128,128]{2,1,0:T(8,128)(2,1)S(1)}, bf16[8,128,128]{2,1,0:T(8,128)(2,1)S(1)}, u32[]{:S(2)}, u32[]{:S(2)}) collective-permute-start(bf16[8,128,128]{2,1,0:T(8,128)(2,1)S(1)} %get-tuple-element.30.k0_ref), channel_id=1, source_target_pairs={{0,192},{1,193},{2,194},{3,195},{4,196},{5,197},{6,198},{7,199},{8... | collective-permute-start | bytes 786440 | tf_op jit(solution)/shard_map/ppermute | solution.py:375
  100.8 82.1 %collective-permute-start.4 = (bf16[8,128,128]{2,1,0:T(8,128)(2,1)S(1)}, bf16[8,128,128]{2,1,0:T(8,128)(2,1)S(1)}, u32[]{:S(2)}, u32[]{:S(2)}) collective-permute-start(bf16[8,128,128]{2,1,0:T(8,128)(2,1)S(1)} %get-tuple-element.30.k0_ref), channel_id=1, source_target_pairs={{0,256},{16,272},{32,288},{48,304},{64,320},{80,336},{96,352},{112... | collective-permute-start | bytes 786440 | tf_op jit(solution)/shard_map/ppermute | solution.py:372
  102.1 87.7 %collective-permute-start.5 = (bf16[8,128,128]{2,1,0:T(8,128)(2,1)S(1)}, bf16[8,128,128]{2,1,0:T(8,128)(2,1)S(1)}, u32[]{:S(2)}, u32[]{:S(2)}) collective-permute-start(bf16[8,128,128]{2,1,0:T(8,128)(2,1)S(1)} %get-tuple-element.30.k0_ref), channel_id=1, source_target_pairs={{0,320},{16,336},{32,352},{48,368},{64,384},{80,400},{96,416},{112... | collective-permute-start | bytes 786440 | tf_op jit(solution)/shard_map/ppermute | solution.py:372
  103.4 93.4 %collective-permute-start.2 = (bf16[8,128,128]{2,1,0:T(8,128)(2,1)S(1)}, bf16[8,128,128]{2,1,0:T(8,128)(2,1)S(1)}, u32[]{:S(2)}, u32[]{:S(2)}) collective-permute-start(bf16[8,128,128]{2,1,0:T(8,128)(2,1)S(1)} %get-tuple-element.30.k0_ref), channel_id=1, source_target_pairs={{0,384},{16,400},{32,416},{48,432},{64,448},{80,464},{96,480},{112... | collective-permute-start | bytes 786440 | tf_op jit(solution)/shard_map/ppermute | solution.py:372
  105.6 98.8 %collective-permute-start.3 = (bf16[8,128,128]{2,1,0:T(8,128)(2,1)S(1)}, bf16[8,128,128]{2,1,0:T(8,128)(2,1)S(1)}, u32[]{:S(2)}, u32[]{:S(2)}) collective-permute-start(bf16[8,128,128]{2,1,0:T(8,128)(2,1)S(1)} %get-tuple-element.30.k0_ref), channel_id=1, source_target_pairs={{0,448},{16,464},{32,480},{48,496},{64,256},{80,272},{96,288},{112... | collective-permute-start | bytes 786440 | tf_op jit(solution)/shard_map/ppermute | solution.py:372
Sparse Core Ops, SparseCore 0:
  9.4 68.1 all-gather.2
where the time goes:
time: 231 us
  waiting for transfers between devices  133 us (58%)
  starting transfers between devices  34.4 us (15%)
  Pallas kernels  27.1 us (12%)
  blocking collectives  14.6 us (6%)
  between operations  14.2 us (6%)
  local copies, waits for them, and re-layouts  5.03 us (2%)
    ppermute x4, waiting for transfers between devices, body(): fars.append(lax.ppermute(kv, CTX, pairs))  81.4 us
    all_to_all x2, waiting for transfers between devices, spread(): return lax.all_to_all(many, axis, 0, 0, tiled=True)  16.6 us
    ppermute x1, waiting for transfers between devices, body(): there = lax.ppermute(tv, 'zh', [(0, 1), (1, 0)])  16.2 us
    all_to_all x1, blocking collectives, body(): lax.all_to_all(last(ids, q, fars[2:], acc, stat), 'x', 0, 0, tiled=True)  14.6 us
    all_to_all x2, starting transfers between devices, spread(): return lax.all_to_all(many, axis, 0, 0, tiled=True)  13.8 us
    all_gather x1, waiting for transfers between devices, body(): mine = lax.all_gather(stream, 'zl', axis=0, tiled=False)  10.5 us
    pallas_call x1, Pallas kernels, project(): pl.pallas_call(project_kernel, out_shape=(jax.ShapeDtypeStruct((4, 4, HD,...  8.64 us
    pallas_call x1, Pallas kernels, near(): pl.pallas_call(near_kernel, out_shape=STATE, in_specs=[SM] + [VM] * 5, ou...  6.5 us
  transfers between devices with their start and end apart: 13, of which 11 were waited for; matrix products, arithmetic and copies ran while one was open for 3% of the time, Pallas kernels for 6%

commit v1 on v0

--- a/solution.py
+++ b/solution.py
@@ -64,7 +64,7 @@
 
 
 def project_kernel(core_ref, mine_ref, other_ref, w_ref, gain_ref, cos_ref, sin_ref,
-                   q_ref, kv_ref, acc_ref):
+                   q_ref, kv_ref, kv0_ref, kv1_ref, acc_ref):
     core = core_ref[0]
     chunk = mine_ref.shape[2]
     per = chunk // HD
@@ -106,8 +106,12 @@
             qt = q[at].T.astype(jnp.bfloat16)
             for copy in range(4):
                 q_ref[copy, 2 * h + half] = qt
+            vt = v[at].T.astype(jnp.bfloat16)
+            one = (kv0_ref, kv1_ref)[h]
             kv_ref[4 * h + half] = k[at]
-            kv_ref[4 * h + 2 + half] = v[at].T.astype(jnp.bfloat16)
+            kv_ref[4 * h + 2 + half] = vt
+            one[half] = k[at]
+            one[2 + half] = vt
 
 
 def project(core, mine, other, w, gain, cosines, sines):
@@ -116,9 +120,11 @@
         out_shape=(
             jax.ShapeDtypeStruct((4, 4, HD, HD), jnp.bfloat16),
             jax.ShapeDtypeStruct((8, HD, HD), jnp.bfloat16),
+            jax.ShapeDtypeStruct((4, HD, HD), jnp.bfloat16),
+            jax.ShapeDtypeStruct((4, HD, HD), jnp.bfloat16),
         ),
         in_specs=[SM] + [VM] * 6,
-        out_specs=(VM, VM),
+        out_specs=(VM,) * 4,
         scratch_shapes=[pltpu.VMEM((TOK, COLS * HD), jnp.float32)],
         compiler_params=params(10),
         name="project",
@@ -195,7 +201,7 @@
 
 def fold(q_ref, refs, n, h, acc, old, total):
     q = load_q(q_ref, n, h)
-    ss = [jnp.dot(load_k(ref, h), q, preferred_element_type=jnp.float32) for ref in refs]
+    ss = [jnp.dot(load_k(ref, 0), q, preferred_element_type=jnp.float32) for ref in refs]
     top = functools.reduce(jnp.maximum, [jnp.max(s, axis=0, keepdims=True) for s in ss], old)
     fac = jnp.exp2((old - top) * SCALE)
     acc = acc * fac
@@ -204,112 +210,71 @@
         p = jnp.exp2((s - top) * SCALE)
         total = total + jnp.sum(p, axis=0, keepdims=True)
         acc = acc + jnp.dot(
-            load_v(ref, h), p.astype(jnp.bfloat16), preferred_element_type=jnp.float32
+            load_v(ref, 0), p.astype(jnp.bfloat16), preferred_element_type=jnp.float32
         )
     return acc, top, total
 
 
-def far_kernel(ids_ref, q_ref, k0_ref, k1_ref, acc_in, stat_in, acc_ref, stat_ref):
+def far_kernel(head, ids_ref, q_ref, kv_ref, acc_ref, stat_ref, *rest):
+    out_ref = rest[-1]
     late = ids_ref[0] > 0
 
-    def one_source(n, c):
-        for h in range(2):
-            i = 2 * n + h
-            acc = acc_in[i]
-            top = stat_in[i, 0:1]
-            total = stat_in[i, 1:2]
-            acc, top, total = fold(q_ref, (k0_ref, k1_ref), n, h, acc, top, total)
-            acc_ref[i] = acc
-            stat_ref[i, 0:1] = top
-            stat_ref[i, 1:2] = total
-        return c
-
-    @pl.when(late)
-    def _():
-        lax.fori_loop(0, 4, one_source, 0)
-
-    @pl.when(jnp.logical_not(late))
-    def _():
-        acc_ref[...] = acc_in[...]
-        stat_ref[...] = stat_in[...]
-
-
-def far(ids, q, fars, acc, stat):
-    return pl.pallas_call(
-        far_kernel,
-        out_shape=STATE,
-        in_specs=[SM] + [VM] * 5,
-        out_specs=(VM, VM),
-        compiler_params=params(10),
-        name="attend_far",
-    )(ids, q, *fars, acc, stat)
-
-
-def last_kernel(ids_ref, q_ref, k0_ref, k1_ref, acc_ref, stat_ref, out_ref):
-    late = ids_ref[0] > 0
-
-    def finish(n, h, acc, top, total):
+    def finish(n, acc, top, total):
         some = total > 0
         safe = jnp.where(some, total, 1.0)
         lse = jnp.where(some, top * SCALE + jnp.log2(safe), NEG)
-        at = slice(h * TOK, (h + 1) * TOK)
-        out_ref[n, 0:HD, at] = (acc / safe).astype(jnp.bfloat16)
+        out_ref[n, head, 0:HD] = (acc / safe).astype(jnp.bfloat16)
         hi = lse.astype(jnp.bfloat16).astype(jnp.float32)
         mid = (lse - hi).astype(jnp.bfloat16).astype(jnp.float32)
         low = lse - hi - mid
         r = lax.broadcasted_iota(jnp.int32, (16, TOK), 0)
         extra = jnp.where(r == 0, hi, jnp.where(r == 1, mid, jnp.where(r == 2, low, 0.0)))
-        out_ref[n, HD:HD + 16, at] = extra.astype(jnp.bfloat16)
-
-    def state(n, h):
-        i = 2 * n + h
+        out_ref[n, head, HD:HD + 16] = extra.astype(jnp.bfloat16)
+
+    def state(n):
+        i = 2 * n + head
         return acc_ref[i], stat_ref[i, 0:1], stat_ref[i, 1:2]
 
     @pl.when(jnp.logical_not(late))
     def _():
-        def one_source(n, c):
-            for h in range(2):
-                finish(n, h, *state(n, h))
-            return c
-
-        lax.fori_loop(0, 4, one_source, 0)
+        for n in range(4):
+            finish(n, *state(n))
 
     @pl.when(late)
     def _():
-        def one_source(n, c):
-            for h in range(2):
-                finish(n, h, *fold(q_ref, (k0_ref, k1_ref), n, h, *state(n, h)))
+        def one_source(m, c):
+            for n in (2 * m, 2 * m + 1):
+                finish(n, *fold(q_ref, [kv_ref.at[k] for k in range(4)], n, head, *state(n)))
             return c
 
-        lax.fori_loop(0, 4, one_source, 0)
-
-
-def last(ids, q, fars, acc, stat):
-    return pl.pallas_call(
-        last_kernel,
-        out_shape=jax.ShapeDtypeStruct((4, HD + 16, 2 * TOK), jnp.bfloat16),
-        in_specs=[SM] + [VM] * 5,
+        lax.fori_loop(0, 2, one_source, 0)
+
+
+def far(head, ids, q, kv, acc, stat, *rest):
+    return pl.pallas_call(
+        functools.partial(far_kernel, head),
+        out_shape=jax.ShapeDtypeStruct((4, 2, HD + 16, TOK), jnp.bfloat16),
+        in_specs=[SM] + [VM] * (4 + len(rest)),
         out_specs=VM,
+        input_output_aliases={5: 0} if rest else {},
         compiler_params=params(10),
-        name="attend_last",
-    )(ids, q, *fars, acc, stat)
+    )(ids, q, kv, acc, stat, *rest)
 
 
 def combine_kernel(parts_ref, out_ref):
-    count = parts_ref.shape[0]
-    lses = []
-    for i in range(count):
-        e = parts_ref[i, HD:HD + 16].astype(jnp.float32)
-        lses.append(e[0:1] + e[1:2] + e[2:3])
-    top = functools.reduce(jnp.maximum, lses)
-    ws = [jnp.exp2(v - top) for v in lses]
-    tot = sum(ws)
-    o = None
-    for i in range(count):
-        t = parts_ref[i, 0:HD].astype(jnp.float32) * (ws[i] / tot)
-        o = t if o is None else o + t
-    out_ref[:, :HD] = o[:, :TOK].T.astype(jnp.bfloat16)
-    out_ref[:, HD:] = o[:, TOK:].T.astype(jnp.bfloat16)
+    for h in range(2):
+        lses = []
+        for i in range(4):
+            e = parts_ref[i, h, HD:HD + 16].astype(jnp.float32)
+            lses.append(e[0:1] + e[1:2] + e[2:3])
+        top = functools.reduce(jnp.maximum, lses)
+        ws = [jnp.exp2(v - top) for v in lses]
+        tot = ws[0] + ws[1] + ws[2] + ws[3]
+        o = None
+        for i in range(4):
+            t = parts_ref[i, h, 0:HD].astype(jnp.float32) * (ws[i] / tot)
+            o = t if o is None else o + t
+        out_ref[:, h * HD:(h + 1) * HD] = o.T.astype(jnp.bfloat16)
 
 
 def combine(parts):
@@ -363,22 +328,21 @@
     )
     other = lax.ppermute(mine, "core", [(0, 1), (1, 0)])
     w = scatter(rows, cols, live, near_tiles, there_tiles)
-    q, kv = project(core.reshape(1), mine, other, w, gain, cosines, sines)
-    fars = []
-    for k in range(4):
-        pairs = [
-            (4 * y + x, 16 + 4 * ((y + k) % 4) + x) for y in range(4) for x in range(4)
-        ]
-        fars.append(lax.ppermute(kv, CTX, pairs))
+    q, kv, kv0, kv1 = project(core.reshape(1), mine, other, w, gain, cosines, sines)
+    across = [(b, 16 + b) for b in range(16)]
+    far0 = lax.ppermute(kv0, CTX, across)
+    far1 = lax.ppermute(kv1, CTX, across)
     keys = [kv]
     for k in range(1, 4):
         keys.append(lax.ppermute(kv, "y", [(y, y + k) for y in range(4 - k)]))
     q = lax.all_to_all(q, "x", 0, 0, tiled=True)
+    far0 = spread(far0, "y", 4)
+    far1 = spread(far1, "y", 4)
     ids = jnp.stack([zh, lax.axis_index("y"), lax.axis_index("x")]).astype(jnp.int32)
     acc, stat = near(ids, q, keys)
-    acc, stat = far(ids, q, fars[:2], acc, stat)
-    parts = lax.all_to_all(last(ids, q, fars[2:], acc, stat), "x", 0, 0, tiled=True)
-    return combine(parts)
+    out = far(0, ids, q, far0, acc, stat)
+    out = far(1, ids, q, far1, acc, stat, out)
+    return combine(lax.all_to_all(out, "x", 0, 0, tiled=True))
 
 
 def solution(mesh):

time: 231 us -> 199 us (0.86)
  the two profiles are of different devices: /device:TPU:472 before, /device:TPU:312 now
where the time goes in v1:
time: 199 us; the launch traced here: 198 us
  waiting for transfers between devices  95.2 us (48%)
  starting transfers between devices  38.3 us (19%)
  Pallas kernels  25.6 us (13%)
  blocking collectives  15.8 us (8%)
  between operations  14.2 us (7%)
  local copies, waits for them, and re-layouts  6.83 us (3%)
  other arithmetic  2.09 us (1%)
    ppermute x1, waiting for transfers between devices, body(): there = lax.ppermute(tv, 'zh', [(0, 1), (1, 0)])  24 us
    all_to_all x4, starting transfers between devices, spread(): return lax.all_to_all(many, axis, 0, 0, tiled=True)  23.9 us
    ppermute x1, waiting for transfers between devices, body(): far0 = lax.ppermute(kv0, CTX, across)  17.4 us
    ppermute x1, waiting for transfers between devices, body(): far1 = lax.ppermute(kv1, CTX, across)  16.5 us
    all_to_all x1, blocking collectives, body(): return combine(lax.all_to_all(out, 'x', 0, 0, tiled=True))  15.8 us
    all_to_all x4, waiting for transfers between devices, spread(): return lax.all_to_all(many, axis, 0, 0, tiled=True)  13.3 us
    ppermute x3, waiting for transfers between devices, body(): keys.append(lax.ppermute(kv, 'y', [(y, y + k) for y in range(4 - k)]))  13.3 us
    all_gather x1, waiting for transfers between devices, body(): mine = lax.all_gather(stream, 'zl', axis=0, tiled=False)  8.7 us
  transfers between devices with their start and end apart: 13, of which 9 were waited for; matrix products, arithmetic and copies ran while one was open for 4% of the time, Pallas kernels for 7%

profile of v1, /device:TPU:312, one launch (start us, length us, event | category | flops | bytes accessed | tf_op | source)
XLA Modules:
  0.0 198.0 jit_solution(7351404092529571783)
XLA Ops:
  7.3 2.4 %broadcast_in_dim.11 = bf16[16,3,128,128]{3,2,1,0:T(8,128)(2,1)} broadcast(bf16[3,128,128]{2,1,0:T(8,128)(2,1)} %bitcast.16), dimensions={1,2,3} | broadcast | bytes 1671168 | tf_op jit(solution)/shard_map/broadcast_in_dim | solution.py:292
  9.7 7.3 %all-to-all-start = ((bf16[16,3,128,128]{3,2,1,0:T(8,128)(2,1)}), bf16[16,3,128,128]{3,2,1,0:T(8,128)(2,1)S(1)}, u32[]{:S(2)}, u32[]{:S(2)}) async-start(bf16[16,3,128,128]{3,2,1,0:T(8,128)(2,1)} %broadcast_in_dim.11), calls=%async_computation | async-start | bytes 3145728 | tf_op jit(solution)/shard_map/all_to_all | solution.py:293
  17.0 1.9 collective-permute-start
  18.9 24.0 %collective-permute-done = bf16[3,128,128]{2,1,0:T(8,128)(2,1)S(1)} collective-permute-done((bf16[3,128,128]{2,1,0:T(8,128)(2,1)S(1)}, bf16[3,128,128]{2,1,0:T(8,128)(2,1)S(1)}, u32[]{:S(2)}, u32[]{:S(2)}) %collective-permute-start) | collective-permute-done | bytes 98336 | tf_op jit(solution)/shard_map/ppermute | solution.py:303
  42.9 1.5 broadcast_in_dim.12
  44.4 7.3 %all-to-all-start.1 = ((bf16[16,3,128,128]{3,2,1,0:T(8,128)(2,1)}), bf16[16,3,128,128]{3,2,1,0:T(8,128)(2,1)S(1)}, u32[]{:S(2)}, u32[]{:S(2)}) async-start(bf16[16,3,128,128]{3,2,1,0:T(8,128)(2,1)} %broadcast_in_dim.12), calls=%async_computation.1 | async-start | bytes 3145728 | tf_op jit(solution)/shard_map/all_to_all | solution.py:293
  55.5 13.3 %all-to-all-done.1 = bf16[16,3,128,128]{3,2,1,0:T(8,128)(2,1)S(1)} async-done(((bf16[16,3,128,128]{3,2,1,0:T(8,128)(2,1)}), bf16[16,3,128,128]{3,2,1,0:T(8,128)(2,1)S(1)}, u32[]{:S(2)}, u32[]{:S(2)}) %all-to-all-start.1) | async-done | bytes 1572896 | tf_op jit(solution)/shard_map/all_to_all | solution.py:293
  68.8 8.7 %all-gather.3.cloned.1.call-done = bf16[2048,512]{1,0:T(8,128)(2,1)} async-done(((bf16[256,512]{1,0:T(8,128)(2,1)}), bf16[2048,512]{1,0:T(8,128)(2,1)}) %all-gather.3.cloned.1.call-update) | async-done | bytes 2097168 | tf_op jit(solution)/shard_map/all_gather | solution.py:301
  77.5 1.9 collective-permute-start.1
  79.5 3.1 %scatter_tiles.1.w_ref = bf16[64,128,768]{2,1,0:T(8,128)(2,1)S(1)} custom-call(s32[96]{0:T(128)S(1)} %reshape.50.row_ref, s32[96]{0:T(128)S(1)} %reshape.51.col_ref, s32[96]{0:T(128)S(1)} %reshape.56.live_ref, bf16[48,128,128]{2,1,0:T(8,128)(2,1)S(1)} %bitcast.11, bf16[48,128,128]{2,1,0:T(8,128)(2,1)S(1)} %bitcast.12), custom_call_target="tpu_custom_call" | custom-call | tf_op jit(solution)/shard_map/scatter_tiles/pallas_call | solution.py:56
  82.6 1.3 collective-permute-done.1.other_ref
  83.9 8.6 %project.1 = (bf16[4,4,128,128]{3,2,1,0:T(8,128)(2,1)}, bf16[8,128,128]{2,1,0:T(8,128)(2,1)S(1)}, bf16[4,128,128]{2,1,0:T(8,128)(2,1)S(1)}, bf16[4,128,128]{2,1,0:T(8,128)(2,1)S(1)}) custom-call(s32[1]{0:T(128)} %bitcast.3.core_ref, bf16[8,256,512]{2,1,0:T(8,128)(2,1)S(1)} %bitcast.14, bf16[8,256,512]{2,1,0:T(8,128)(2,1)} %collective-permute-done.1.other_ref, ...), custom_call_target="tpu_custom_call" | custom-call | tf_op jit(solution)/shard_map/project/pallas_call | solution.py:118
  92.6 4.1 %all-to-all-start.2 = ((bf16[4,4,128,128]{3,2,1,0:T(8,128)(2,1)}), bf16[4,4,128,128]{3,2,1,0:T(8,128)(2,1)S(1)}, u32[]{:S(2)}, u32[]{:S(2)}) async-start(bf16[4,4,128,128]{3,2,1,0:T(8,128)(2,1)} %get-tuple-element.29), calls=%async_computation.2 | async-start | bytes 1048576 | tf_op jit(solution)/shard_map/all_to_all | solution.py:338
  96.7 1.3 collective-permute-start.6
  98.0 17.4 %collective-permute-done.6 = bf16[4,128,128]{2,1,0:T(8,128)(2,1)S(1)} collective-permute-done((bf16[4,128,128]{2,1,0:T(8,128)(2,1)S(1)}, bf16[4,128,128]{2,1,0:T(8,128)(2,1)S(1)}, u32[]{:S(2)}, u32[]{:S(2)}) %collective-permute-start.6) | collective-permute-done | bytes 131104 | tf_op jit(solution)/shard_map/ppermute | solution.py:333
  115.3 0.9 broadcast_in_dim.14
  116.2 4.5 %all-to-all-start.4 = ((bf16[4,4,128,128]{3,2,1,0:T(8,128)(2,1)}), bf16[4,4,128,128]{3,2,1,0:T(8,128)(2,1)S(1)}, u32[]{:S(2)}, u32[]{:S(2)}) async-start(bf16[4,4,128,128]{3,2,1,0:T(8,128)(2,1)} %broadcast_in_dim.14), calls=%async_computation.4 | async-start | bytes 1048576 | tf_op jit(solution)/shard_map/all_to_all | solution.py:293
  120.7 1.3 collective-permute-start.2
  122.0 16.5 %collective-permute-done.2 = bf16[4,128,128]{2,1,0:T(8,128)(2,1)S(1)} collective-permute-done((bf16[4,128,128]{2,1,0:T(8,128)(2,1)S(1)}, bf16[4,128,128]{2,1,0:T(8,128)(2,1)S(1)}, u32[]{:S(2)}, u32[]{:S(2)}) %collective-permute-start.2) | collective-permute-done | bytes 131104 | tf_op jit(solution)/shard_map/ppermute | solution.py:334
  138.5 0.9 broadcast_in_dim.13
  139.4 4.8 %all-to-all-start.3 = ((bf16[4,4,128,128]{3,2,1,0:T(8,128)(2,1)}), bf16[4,4,128,128]{3,2,1,0:T(8,128)(2,1)S(1)}, u32[]{:S(2)}, u32[]{:S(2)}) async-start(bf16[4,4,128,128]{3,2,1,0:T(8,128)(2,1)} %broadcast_in_dim.13), calls=%async_computation.3 | async-start | bytes 1048576 | tf_op jit(solution)/shard_map/all_to_all | solution.py:293
  144.2 1.3 collective-permute-start.3
  145.5 1.3 collective-permute-start.4
  146.8 1.3 collective-permute-start.5
  148.2 6.7 %collective-permute-done.3.k1_ref = bf16[8,128,128]{2,1,0:T(8,128)(2,1)S(1)} collective-permute-done((bf16[8,128,128]{2,1,0:T(8,128)(2,1)S(1)}, bf16[8,128,128]{2,1,0:T(8,128)(2,1)S(1)}, u32[]{:S(2)}, u32[]{:S(2)}) %collective-permute-start.3) | collective-permute-done | bytes 262176 | tf_op jit(solution)/shard_map/ppermute | solution.py:337
  154.9 1.1 collective-permute-done.4.k2_ref
  155.9 5.5 %collective-permute-done.5.k3_ref = bf16[8,128,128]{2,1,0:T(8,128)(2,1)S(1)} collective-permute-done((bf16[8,128,128]{2,1,0:T(8,128)(2,1)S(1)}, bf16[8,128,128]{2,1,0:T(8,128)(2,1)S(1)}, u32[]{:S(2)}, u32[]{:S(2)}) %collective-permute-start.5) | collective-permute-done | bytes 262176 | tf_op jit(solution)/shard_map/ppermute | solution.py:337
  161.5 6.6 %attend_near.1 = (f32[8,128,256]{2,1,0:T(8,128)S(1)}, f32[8,8,256]{2,1,0:T(8,128)S(1)}) custom-call(s32[3]{0:T(128)S(1)} %pad_add_fusion.ids_ref, bf16[4,4,128,128]{3,2,1,0:T(8,128)(2,1)S(1)} %all-to-all-done.2.q_ref, bf16[8,128,128]{2,1,0:T(8,128)(2,1)S(1)} %get-tuple-element.31.k0_ref, bf16[8,128,128]{2,1,0:T(8,128)(2,1)S(1)} %collective-permute-done.3.k1_ref, ...), custom_call_target="tpu_custom_call" | custom-call | tf_op jit(solution)/shard_map/attend_near/pallas_call | solution.py:192
  168.0 3.2 %shard_map.64.rest_0_ = bf16[4,2,144,256]{3,2,1,0:T(8,128)(2,1)S(1)} custom-call(s32[3]{0:T(128)S(1)} %pad_add_fusion.ids_ref, bf16[4,4,128,128]{3,2,1,0:T(8,128)(2,1)S(1)} %all-to-all-done.2.q_ref, bf16[4,4,128,128]{3,2,1,0:T(8,128)(2,1)S(1)} %all-to-all-done.4.kv_ref, f32[8,128,256]{2,1,0:T(8,128)S(1)} %get-tuple-element.32.acc_ref, ...), custom_call_target="tpu_custom_call" | custom-call | tf_op jit(solution)/shard_map/pallas_call | solution.py:254
  171.3 3.2 %shard_map.65 = bf16[4,2,144,256]{3,2,1,0:T(8,128)(2,1)S(1)} custom-call(s32[3]{0:T(128)S(1)} %pad_add_fusion.ids_ref, bf16[4,4,128,128]{3,2,1,0:T(8,128)(2,1)S(1)} %all-to-all-done.2.q_ref, bf16[4,4,128,128]{3,2,1,0:T(8,128)(2,1)S(1)} %all-to-all-done.3.kv_ref, f32[8,128,256]{2,1,0:T(8,128)S(1)} %get-tuple-element.32.acc_ref, ...), custom_call_target="tpu_custom_call", output_to_operand_aliasing={{}: (5, {})} | custom-call | tf_op jit(solution)/shard_map/pallas_call | solution.py:254
  174.5 15.8 %all_to_all.30.parts_ref = bf16[4,2,144,256]{3,2,1,0:T(8,128)(2,1)S(1)} all-to-all(bf16[4,2,144,256]{3,2,1,0:T(8,128)(2,1)S(1)} %shard_map.65), channel_id=1, replica_groups=mesh['zh'=2,'y'=4,'x'=4,'zl'=8,'core'=2] {'x'}, dimensions={0} | all-to-all | bytes 1179648 | tf_op jit(solution)/shard_map/all_to_all | solution.py:345
  190.3 0.9 combine.1
  (35 shorter events, 3.9 us)
Async XLA Ops:
  6.5 71.0 %all-gather.3.cloned.1.call-start = ((), (), s32[]{:S(2)}) async-start(), calls=%async_computation.6 | async-start | bytes 2359296 | tf_op jit(solution)/shard_map/all_gather | solution.py:301
  9.7 7.3 %copy-start.2 = (bf16[1,3,128,128]{3,2,1,0:T(8,128)(2,1)S(1)}, bf16[1,3,128,128]{3,2,1,0:T(8,128)(2,1)}, u32[]{:S(2)}) copy-start(bf16[1,3,128,128]{3,2,1,0:T(8,128)(2,1)} %param.8) | copy-start | bytes 294916
  9.7 33.2 %all-to-all-start = ((bf16[16,3,128,128]{3,2,1,0:T(8,128)(2,1)}), bf16[16,3,128,128]{3,2,1,0:T(8,128)(2,1)S(1)}, u32[]{:S(2)}, u32[]{:S(2)}) async-start(bf16[16,3,128,128]{3,2,1,0:T(8,128)(2,1)} %broadcast_in_dim.11), calls=%async_computation | async-start | bytes 3145728 | tf_op jit(solution)/shard_map/all_to_all | solution.py:293
  17.0 25.9 %collective-permute-start = (bf16[3,128,128]{2,1,0:T(8,128)(2,1)S(1)}, bf16[3,128,128]{2,1,0:T(8,128)(2,1)S(1)}, u32[]{:S(2)}, u32[]{:S(2)}) collective-permute-start(bf16[3,128,128]{2,1,0:T(8,128)(2,1)S(1)} %bitcast.17), channel_id=1, source_target_pairs={{0,256},{256,0},{1,257},{257,1},{2,258},{258,2},{3,259},{259,3},{4... | collective-permute-start | bytes 294920 | tf_op jit(solution)/shard_map/ppermute | solution.py:303
  44.4 7.9 %copy-start.3 = (s32[1,96]{1,0:T(1,128)S(1)}, s32[1,96]{1,0:T(1,128)}, u32[]{:S(2)}) copy-start(s32[1,96]{1,0:T(1,128)} %param.10) | copy-start | bytes 1156
  44.4 8.7 %copy-start.4 = (s32[1,96]{1,0:T(1,128)S(1)}, s32[1,96]{1,0:T(1,128)}, u32[]{:S(2)}) copy-start(s32[1,96]{1,0:T(1,128)} %param.9) | copy-start | bytes 1156
  44.4 24.4 %all-to-all-start.1 = ((bf16[16,3,128,128]{3,2,1,0:T(8,128)(2,1)}), bf16[16,3,128,128]{3,2,1,0:T(8,128)(2,1)S(1)}, u32[]{:S(2)}, u32[]{:S(2)}) async-start(bf16[16,3,128,128]{3,2,1,0:T(8,128)(2,1)} %broadcast_in_dim.12), calls=%async_computation.1 | async-start | bytes 3145728 | tf_op jit(solution)/shard_map/all_to_all | solution.py:293
  77.5 6.4 %collective-permute-start.1 = (bf16[8,256,512]{2,1,0:T(8,128)(2,1)}, bf16[8,256,512]{2,1,0:T(8,128)(2,1)}, u32[]{:S(2)}, u32[]{:S(2)}) collective-permute-start(bf16[8,256,512]{2,1,0:T(8,128)(2,1)} %bitcast.13), channel_id=1, source_target_pairs={{0,1},{1,0},{2,3},{3,2},{4,5},{5,4},{6,7},{7,6},{8,9},{9,8},{10,11... | collective-permute-start | bytes 6291464 | tf_op jit(solution)/shard_map/ppermute | solution.py:329
  79.4 4.5 %copy-start = (bf16[2048,512]{1,0:T(8,128)(2,1)S(1)}, bf16[2048,512]{1,0:T(8,128)(2,1)}, u32[]{:S(2)}) copy-start(bf16[2048,512]{1,0:T(8,128)(2,1)} %all-gather.3.cloned.1.call-done) | copy-start | bytes 6291460
  79.4 4.5 %copy-start.1 = (f32[8192]{0:T(1024)S(1)}, f32[8192]{0:T(1024)}, u32[]{:S(2)}) copy-start(f32[8192]{0:T(1024)} %param.7) | copy-start | bytes 98308
  92.6 22.8 %all-to-all-start.2 = ((bf16[4,4,128,128]{3,2,1,0:T(8,128)(2,1)}), bf16[4,4,128,128]{3,2,1,0:T(8,128)(2,1)S(1)}, u32[]{:S(2)}, u32[]{:S(2)}) async-start(bf16[4,4,128,128]{3,2,1,0:T(8,128)(2,1)} %get-tuple-element.29), calls=%async_computation.2 | async-start | bytes 1048576 | tf_op jit(solution)/shard_map/all_to_all | solution.py:338
  96.7 18.7 %collective-permute-start.6 = (bf16[4,128,128]{2,1,0:T(8,128)(2,1)S(1)}, bf16[4,128,128]{2,1,0:T(8,128)(2,1)S(1)}, u32[]{:S(2)}, u32[]{:S(2)}) collective-permute-start(bf16[4,128,128]{2,1,0:T(8,128)(2,1)S(1)} %get-tuple-element.34), channel_id=1, source_target_pairs={{0,256},{16,272},{32,288},{48,304},{64,320},{80,336},{96,352},{112... | collective-permute-start | bytes 393224 | tf_op jit(solution)/shard_map/ppermute | solution.py:333
  116.2 22.3 %all-to-all-start.4 = ((bf16[4,4,128,128]{3,2,1,0:T(8,128)(2,1)}), bf16[4,4,128,128]{3,2,1,0:T(8,128)(2,1)S(1)}, u32[]{:S(2)}, u32[]{:S(2)}) async-start(bf16[4,4,128,128]{3,2,1,0:T(8,128)(2,1)} %broadcast_in_dim.14), calls=%async_computation.4 | async-start | bytes 1048576 | tf_op jit(solution)/shard_map/all_to_all | solution.py:293
  120.7 17.8 %collective-permute-start.2 = (bf16[4,128,128]{2,1,0:T(8,128)(2,1)S(1)}, bf16[4,128,128]{2,1,0:T(8,128)(2,1)S(1)}, u32[]{:S(2)}, u32[]{:S(2)}) collective-permute-start(bf16[4,128,128]{2,1,0:T(8,128)(2,1)S(1)} %get-tuple-element.30), channel_id=1, source_target_pairs={{0,256},{16,272},{32,288},{48,304},{64,320},{80,336},{96,352},{112... | collective-permute-start | bytes 393224 | tf_op jit(solution)/shard_map/ppermute | solution.py:334
  139.4 31.8 %all-to-all-start.3 = ((bf16[4,4,128,128]{3,2,1,0:T(8,128)(2,1)}), bf16[4,4,128,128]{3,2,1,0:T(8,128)(2,1)S(1)}, u32[]{:S(2)}, u32[]{:S(2)}) async-start(bf16[4,4,128,128]{3,2,1,0:T(8,128)(2,1)} %broadcast_in_dim.13), calls=%async_computation.3 | async-start | bytes 1048576 | tf_op jit(solution)/shard_map/all_to_all | solution.py:293
  144.2 10.7 %collective-permute-start.3 = (bf16[8,128,128]{2,1,0:T(8,128)(2,1)S(1)}, bf16[8,128,128]{2,1,0:T(8,128)(2,1)S(1)}, u32[]{:S(2)}, u32[]{:S(2)}) collective-permute-start(bf16[8,128,128]{2,1,0:T(8,128)(2,1)S(1)} %get-tuple-element.31.k0_ref), channel_id=1, source_target_pairs={{0,64},{64,128},{128,192},{1,65},{65,129},{129,193},{2,66},{66,130... | collective-permute-start | bytes 786440 | tf_op jit(solution)/shard_map/ppermute | solution.py:337
  145.5 10.4 %collective-permute-start.4 = (bf16[8,128,128]{2,1,0:T(8,128)(2,1)S(1)}, bf16[8,128,128]{2,1,0:T(8,128)(2,1)S(1)}, u32[]{:S(2)}, u32[]{:S(2)}) collective-permute-start(bf16[8,128,128]{2,1,0:T(8,128)(2,1)S(1)} %get-tuple-element.31.k0_ref), channel_id=1, source_target_pairs={{0,128},{64,192},{1,129},{65,193},{2,130},{66,194},{3,131},{67,195... | collective-permute-start | bytes 786440 | tf_op jit(solution)/shard_map/ppermute | solution.py:337
  146.8 14.7 %collective-permute-start.5 = (bf16[8,128,128]{2,1,0:T(8,128)(2,1)S(1)}, bf16[8,128,128]{2,1,0:T(8,128)(2,1)S(1)}, u32[]{:S(2)}, u32[]{:S(2)}) collective-permute-start(bf16[8,128,128]{2,1,0:T(8,128)(2,1)S(1)} %get-tuple-element.31.k0_ref), channel_id=1, source_target_pairs={{0,192},{1,193},{2,194},{3,195},{4,196},{5,197},{6,198},{7,199},{8... | collective-permute-start | bytes 786440 | tf_op jit(solution)/shard_map/ppermute | solution.py:337
Sparse Core Ops, SparseCore 0:
  9.4 68.0 all-gather.2

commit v2 on v1

--- a/solution.py
+++ b/solution.py
@@ -30,6 +30,10 @@
     return pltpu.CompilerParams(vmem_limit_bytes=mib * 1024 * 1024)
 
 
+def line_at(i):
+    return 2 * i if i < 4 else 15 - 2 * i
+
+
 def scatter_kernel(row_ref, col_ref, live_ref, near_ref, there_ref, w_ref):
     def clear(i, c):
         w_ref[i] = jnp.zeros((HD, COLS * HD), jnp.bfloat16)
@@ -81,16 +85,17 @@
     acc_ref[...] = jnp.zeros_like(acc_ref)
 
     def step(i, c):
+        at = jnp.where(i < 4, 2 * i, 15 - 2 * i)
         part = None
         for ref, cc in ((mine_ref, core), (other_ref, 1 - core)):
-            x = ref[i].astype(jnp.float32) * r * gain_ref[2 * i + cc]
-            w = w_ref[pl.ds((2 * i + cc) * per, per)].reshape(chunk, COLS * HD)
+            x = ref[i].astype(jnp.float32) * r * gain_ref[2 * at + cc]
+            w = w_ref[pl.ds((2 * at + cc) * per, per)].reshape(chunk, COLS * HD)
             d = jnp.dot(x.astype(jnp.bfloat16), w, preferred_element_type=jnp.float32)
             part = d if part is None else part + d
         acc_ref[...] += part
         return c
 
-    lax.fori_loop(0, 8, step, 0)
+    lax.fori_loop(0, 8, step, 0, unroll=4)
     cosines = cos_ref[...]
     sines = sin_ref[...]
 
@@ -298,7 +303,9 @@
     core = lax.axis_index("core")
     plane = lax.axis_index(PLANE)
     block = zh * 16 + plane
-    mine = lax.all_gather(stream, "zl", axis=0, tiled=False)
+    mine = lax.all_gather(
+        stream, "zl", axis=0, tiled=False, axis_index_groups=[[line_at(i) for i in range(8)]]
+    )
     tv = tile_vals[0]
     there = lax.ppermute(tv, "zh", [(0, 1), (1, 0)])
     near_tiles = spread(tv, PLANE, 16).reshape(-1, HD, HD)

time: 199 us -> 196 us (0.985)
  the two profiles are of different devices: /device:TPU:312 before, /device:TPU:376 now
where the time goes in v2:
time: 196 us; the launch traced here: 195 us
  waiting for transfers between devices  94.4 us (48%)
  starting transfers between devices  38.8 us (20%)
  Pallas kernels  24.5 us (12%)
  blocking collectives  14.7 us (8%)
  between operations  14.2 us (7%)
  local copies, waits for them, and re-layouts  6.83 us (3%)
  other arithmetic  2.09 us (1%)
    all_to_all x4, starting transfers between devices, spread(): return lax.all_to_all(many, axis, 0, 0, tiled=True)  24.3 us
    ppermute x1, waiting for transfers between devices, body(): there = lax.ppermute(tv, 'zh', [(0, 1), (1, 0)])  23.9 us
    ppermute x1, waiting for transfers between devices, body(): far0 = lax.ppermute(kv0, CTX, across)  20.3 us
    ppermute x1, waiting for transfers between devices, body(): far1 = lax.ppermute(kv1, CTX, across)  15.8 us
    ppermute x3, waiting for transfers between devices, body(): keys.append(lax.ppermute(kv, 'y', [(y, y + k) for y in range(4 - k)]))  14.8 us
    all_to_all x1, blocking collectives, body(): return combine(lax.all_to_all(out, 'x', 0, 0, tiled=True))  14.7 us
    all_to_all x4, waiting for transfers between devices, spread(): return lax.all_to_all(many, axis, 0, 0, tiled=True)  14.3 us
    pallas_call x1, Pallas kernels, project(): pl.pallas_call(project_kernel, out_shape=(jax.ShapeDtypeStruct((4, 4, HD,...  7.48 us
  transfers between devices with their start and end apart: 13, of which 9 were waited for; matrix products, arithmetic and copies ran while one was open for 4% of the time, Pallas kernels for 7%

profile of v2, /device:TPU:376, one launch (start us, length us, event | category | flops | bytes accessed | tf_op | source)
XLA Modules:
  0.0 195.5 jit_solution(8018145354467092351)
XLA Ops:
  6.5 0.7 all-gather.3.cloned.1.call-update
  7.3 2.4 %broadcast_in_dim.11 = bf16[16,3,128,128]{3,2,1,0:T(8,128)(2,1)} broadcast(bf16[3,128,128]{2,1,0:T(8,128)(2,1)} %bitcast.16), dimensions={1,2,3} | broadcast | bytes 1671168 | tf_op jit(solution)/shard_map/broadcast_in_dim | solution.py:297
  9.7 7.3 %all-to-all-start = ((bf16[16,3,128,128]{3,2,1,0:T(8,128)(2,1)}), bf16[16,3,128,128]{3,2,1,0:T(8,128)(2,1)S(1)}, u32[]{:S(2)}, u32[]{:S(2)}) async-start(bf16[16,3,128,128]{3,2,1,0:T(8,128)(2,1)} %broadcast_in_dim.11), calls=%async_computation | async-start | bytes 3145728 | tf_op jit(solution)/shard_map/all_to_all | solution.py:298
  17.0 1.9 collective-permute-start
  18.9 23.9 %collective-permute-done = bf16[3,128,128]{2,1,0:T(8,128)(2,1)S(1)} collective-permute-done((bf16[3,128,128]{2,1,0:T(8,128)(2,1)S(1)}, bf16[3,128,128]{2,1,0:T(8,128)(2,1)S(1)}, u32[]{:S(2)}, u32[]{:S(2)}) %collective-permute-start) | collective-permute-done | bytes 98336 | tf_op jit(solution)/shard_map/ppermute | solution.py:310
  42.9 1.5 broadcast_in_dim.12
  44.4 7.4 %all-to-all-start.1 = ((bf16[16,3,128,128]{3,2,1,0:T(8,128)(2,1)}), bf16[16,3,128,128]{3,2,1,0:T(8,128)(2,1)S(1)}, u32[]{:S(2)}, u32[]{:S(2)}) async-start(bf16[16,3,128,128]{3,2,1,0:T(8,128)(2,1)} %broadcast_in_dim.12), calls=%async_computation.1 | async-start | bytes 3145728 | tf_op jit(solution)/shard_map/all_to_all | solution.py:298
  55.5 14.3 %all-to-all-done.1 = bf16[16,3,128,128]{3,2,1,0:T(8,128)(2,1)S(1)} async-done(((bf16[16,3,128,128]{3,2,1,0:T(8,128)(2,1)}), bf16[16,3,128,128]{3,2,1,0:T(8,128)(2,1)S(1)}, u32[]{:S(2)}, u32[]{:S(2)}) %all-to-all-start.1) | async-done | bytes 1572896 | tf_op jit(solution)/shard_map/all_to_all | solution.py:298
  69.8 3.3 %all-gather.3.cloned.1.call-done = bf16[2048,512]{1,0:T(8,128)(2,1)} async-done(((bf16[256,512]{1,0:T(8,128)(2,1)}), bf16[2048,512]{1,0:T(8,128)(2,1)}) %all-gather.3.cloned.1.call-update) | async-done | bytes 2097168 | tf_op jit(solution)/shard_map/all_gather | solution.py:306
  73.1 1.9 collective-permute-start.1
  75.1 3.2 %scatter_tiles.1.w_ref = bf16[64,128,768]{2,1,0:T(8,128)(2,1)S(1)} custom-call(s32[96]{0:T(128)S(1)} %reshape.50.row_ref, s32[96]{0:T(128)S(1)} %reshape.51.col_ref, s32[96]{0:T(128)S(1)} %reshape.56.live_ref, bf16[48,128,128]{2,1,0:T(8,128)(2,1)S(1)} %bitcast.11, bf16[48,128,128]{2,1,0:T(8,128)(2,1)S(1)} %bitcast.12), custom_call_target="tpu_custom_call" | custom-call | tf_op jit(solution)/shard_map/scatter_tiles/pallas_call | solution.py:60
  78.3 1.3 collective-permute-done.1.other_ref
  79.5 7.5 %project.1 = (bf16[4,4,128,128]{3,2,1,0:T(8,128)(2,1)}, bf16[8,128,128]{2,1,0:T(8,128)(2,1)S(1)}, bf16[4,128,128]{2,1,0:T(8,128)(2,1)S(1)}, bf16[4,128,128]{2,1,0:T(8,128)(2,1)S(1)}) custom-call(s32[1]{0:T(128)} %bitcast.3.core_ref, bf16[8,256,512]{2,1,0:T(8,128)(2,1)S(1)} %bitcast.14, bf16[8,256,512]{2,1,0:T(8,128)(2,1)} %collective-permute-done.1.other_ref, ...), custom_call_target="tpu_custom_call" | custom-call | tf_op jit(solution)/shard_map/project/pallas_call | solution.py:123
  87.0 4.2 %all-to-all-start.2 = ((bf16[4,4,128,128]{3,2,1,0:T(8,128)(2,1)}), bf16[4,4,128,128]{3,2,1,0:T(8,128)(2,1)S(1)}, u32[]{:S(2)}, u32[]{:S(2)}) async-start(bf16[4,4,128,128]{3,2,1,0:T(8,128)(2,1)} %get-tuple-element.29), calls=%async_computation.2 | async-start | bytes 1048576 | tf_op jit(solution)/shard_map/all_to_all | solution.py:345
  91.2 1.3 collective-permute-start.6
  92.5 20.3 %collective-permute-done.6 = bf16[4,128,128]{2,1,0:T(8,128)(2,1)S(1)} collective-permute-done((bf16[4,128,128]{2,1,0:T(8,128)(2,1)S(1)}, bf16[4,128,128]{2,1,0:T(8,128)(2,1)S(1)}, u32[]{:S(2)}, u32[]{:S(2)}) %collective-permute-start.6) | collective-permute-done | bytes 131104 | tf_op jit(solution)/shard_map/ppermute | solution.py:340
  112.8 0.9 broadcast_in_dim.14
  113.7 4.8 %all-to-all-start.4 = ((bf16[4,4,128,128]{3,2,1,0:T(8,128)(2,1)}), bf16[4,4,128,128]{3,2,1,0:T(8,128)(2,1)S(1)}, u32[]{:S(2)}, u32[]{:S(2)}) async-start(bf16[4,4,128,128]{3,2,1,0:T(8,128)(2,1)} %broadcast_in_dim.14), calls=%async_computation.4 | async-start | bytes 1048576 | tf_op jit(solution)/shard_map/all_to_all | solution.py:298
  118.5 1.3 collective-permute-start.2
  119.8 15.8 %collective-permute-done.2 = bf16[4,128,128]{2,1,0:T(8,128)(2,1)S(1)} collective-permute-done((bf16[4,128,128]{2,1,0:T(8,128)(2,1)S(1)}, bf16[4,128,128]{2,1,0:T(8,128)(2,1)S(1)}, u32[]{:S(2)}, u32[]{:S(2)}) %collective-permute-start.2) | collective-permute-done | bytes 131104 | tf_op jit(solution)/shard_map/ppermute | solution.py:341
  135.6 0.9 broadcast_in_dim.13
  136.5 4.8 %all-to-all-start.3 = ((bf16[4,4,128,128]{3,2,1,0:T(8,128)(2,1)}), bf16[4,4,128,128]{3,2,1,0:T(8,128)(2,1)S(1)}, u32[]{:S(2)}, u32[]{:S(2)}) async-start(bf16[4,4,128,128]{3,2,1,0:T(8,128)(2,1)} %broadcast_in_dim.13), calls=%async_computation.3 | async-start | bytes 1048576 | tf_op jit(solution)/shard_map/all_to_all | solution.py:298
  141.3 1.3 collective-permute-start.3
  142.6 1.3 collective-permute-start.4
  143.9 1.3 collective-permute-start.5
  145.3 8.5 %collective-permute-done.3.k1_ref = bf16[8,128,128]{2,1,0:T(8,128)(2,1)S(1)} collective-permute-done((bf16[8,128,128]{2,1,0:T(8,128)(2,1)S(1)}, bf16[8,128,128]{2,1,0:T(8,128)(2,1)S(1)}, u32[]{:S(2)}, u32[]{:S(2)}) %collective-permute-start.3) | collective-permute-done | bytes 262176 | tf_op jit(solution)/shard_map/ppermute | solution.py:344
  154.5 5.5 %collective-permute-done.5.k3_ref = bf16[8,128,128]{2,1,0:T(8,128)(2,1)S(1)} collective-permute-done((bf16[8,128,128]{2,1,0:T(8,128)(2,1)S(1)}, bf16[8,128,128]{2,1,0:T(8,128)(2,1)S(1)}, u32[]{:S(2)}, u32[]{:S(2)}) %collective-permute-start.5) | collective-permute-done | bytes 262176 | tf_op jit(solution)/shard_map/ppermute | solution.py:344
  160.1 6.6 %attend_near.1 = (f32[8,128,256]{2,1,0:T(8,128)S(1)}, f32[8,8,256]{2,1,0:T(8,128)S(1)}) custom-call(s32[3]{0:T(128)S(1)} %pad_add_fusion.ids_ref, bf16[4,4,128,128]{3,2,1,0:T(8,128)(2,1)S(1)} %all-to-all-done.2.q_ref, bf16[8,128,128]{2,1,0:T(8,128)(2,1)S(1)} %get-tuple-element.31.k0_ref, bf16[8,128,128]{2,1,0:T(8,128)(2,1)S(1)} %collective-permute-done.3.k1_ref, ...), custom_call_target="tpu_custom_call" | custom-call | tf_op jit(solution)/shard_map/attend_near/pallas_call | solution.py:197
  166.6 3.2 %shard_map.64.rest_0_ = bf16[4,2,144,256]{3,2,1,0:T(8,128)(2,1)S(1)} custom-call(s32[3]{0:T(128)S(1)} %pad_add_fusion.ids_ref, bf16[4,4,128,128]{3,2,1,0:T(8,128)(2,1)S(1)} %all-to-all-done.2.q_ref, bf16[4,4,128,128]{3,2,1,0:T(8,128)(2,1)S(1)} %all-to-all-done.4.kv_ref, f32[8,128,256]{2,1,0:T(8,128)S(1)} %get-tuple-element.32.acc_ref, ...), custom_call_target="tpu_custom_call" | custom-call | tf_op jit(solution)/shard_map/pallas_call | solution.py:259
  169.9 3.2 %shard_map.65 = bf16[4,2,144,256]{3,2,1,0:T(8,128)(2,1)S(1)} custom-call(s32[3]{0:T(128)S(1)} %pad_add_fusion.ids_ref, bf16[4,4,128,128]{3,2,1,0:T(8,128)(2,1)S(1)} %all-to-all-done.2.q_ref, bf16[4,4,128,128]{3,2,1,0:T(8,128)(2,1)S(1)} %all-to-all-done.3.kv_ref, f32[8,128,256]{2,1,0:T(8,128)S(1)} %get-tuple-element.32.acc_ref, ...), custom_call_target="tpu_custom_call", output_to_operand_aliasing={{}: (5, {})} | custom-call | tf_op jit(solution)/shard_map/pallas_call | solution.py:259
  173.1 14.7 %all_to_all.30.parts_ref = bf16[4,2,144,256]{3,2,1,0:T(8,128)(2,1)S(1)} all-to-all(bf16[4,2,144,256]{3,2,1,0:T(8,128)(2,1)S(1)} %shard_map.65), channel_id=1, replica_groups=mesh['zh'=2,'y'=4,'x'=4,'zl'=8,'core'=2] {'x'}, dimensions={0} | all-to-all | bytes 1179648 | tf_op jit(solution)/shard_map/all_to_all | solution.py:352
  187.8 0.9 combine.1
  (35 shorter events, 3.9 us)
Async XLA Ops:
  6.5 66.6 %all-gather.3.cloned.1.call-start = ((), (), s32[]{:S(2)}) async-start(), calls=%async_computation.6 | async-start | bytes 2359296 | tf_op jit(solution)/shard_map/all_gather | solution.py:306
  9.7 7.3 %copy-start.2 = (bf16[1,3,128,128]{3,2,1,0:T(8,128)(2,1)S(1)}, bf16[1,3,128,128]{3,2,1,0:T(8,128)(2,1)}, u32[]{:S(2)}) copy-start(bf16[1,3,128,128]{3,2,1,0:T(8,128)(2,1)} %param.8) | copy-start | bytes 294916
  9.7 33.2 %all-to-all-start = ((bf16[16,3,128,128]{3,2,1,0:T(8,128)(2,1)}), bf16[16,3,128,128]{3,2,1,0:T(8,128)(2,1)S(1)}, u32[]{:S(2)}, u32[]{:S(2)}) async-start(bf16[16,3,128,128]{3,2,1,0:T(8,128)(2,1)} %broadcast_in_dim.11), calls=%async_computation | async-start | bytes 3145728 | tf_op jit(solution)/shard_map/all_to_all | solution.py:298
  17.0 25.9 %collective-permute-start = (bf16[3,128,128]{2,1,0:T(8,128)(2,1)S(1)}, bf16[3,128,128]{2,1,0:T(8,128)(2,1)S(1)}, u32[]{:S(2)}, u32[]{:S(2)}) collective-permute-start(bf16[3,128,128]{2,1,0:T(8,128)(2,1)S(1)} %bitcast.17), channel_id=1, source_target_pairs={{0,256},{256,0},{1,257},{257,1},{2,258},{258,2},{3,259},{259,3},{4... | collective-permute-start | bytes 294920 | tf_op jit(solution)/shard_map/ppermute | solution.py:310
  44.4 8.0 %copy-start.3 = (s32[1,96]{1,0:T(1,128)S(1)}, s32[1,96]{1,0:T(1,128)}, u32[]{:S(2)}) copy-start(s32[1,96]{1,0:T(1,128)} %param.10) | copy-start | bytes 1156
  44.4 8.7 %copy-start.4 = (s32[1,96]{1,0:T(1,128)S(1)}, s32[1,96]{1,0:T(1,128)}, u32[]{:S(2)}) copy-start(s32[1,96]{1,0:T(1,128)} %param.9) | copy-start | bytes 1156
  44.4 25.4 %all-to-all-start.1 = ((bf16[16,3,128,128]{3,2,1,0:T(8,128)(2,1)}), bf16[16,3,128,128]{3,2,1,0:T(8,128)(2,1)S(1)}, u32[]{:S(2)}, u32[]{:S(2)}) async-start(bf16[16,3,128,128]{3,2,1,0:T(8,128)(2,1)} %broadcast_in_dim.12), calls=%async_computation.1 | async-start | bytes 3145728 | tf_op jit(solution)/shard_map/all_to_all | solution.py:298
  73.1 6.4 %collective-permute-start.1 = (bf16[8,256,512]{2,1,0:T(8,128)(2,1)}, bf16[8,256,512]{2,1,0:T(8,128)(2,1)}, u32[]{:S(2)}, u32[]{:S(2)}) collective-permute-start(bf16[8,256,512]{2,1,0:T(8,128)(2,1)} %bitcast.13), channel_id=1, source_target_pairs={{0,1},{1,0},{2,3},{3,2},{4,5},{5,4},{6,7},{7,6},{8,9},{9,8},{10,11... | collective-permute-start | bytes 6291464 | tf_op jit(solution)/shard_map/ppermute | solution.py:336
  75.0 4.5 %copy-start = (bf16[2048,512]{1,0:T(8,128)(2,1)S(1)}, bf16[2048,512]{1,0:T(8,128)(2,1)}, u32[]{:S(2)}) copy-start(bf16[2048,512]{1,0:T(8,128)(2,1)} %all-gather.3.cloned.1.call-done) | copy-start | bytes 6291460
  75.0 4.5 %copy-start.1 = (f32[8192]{0:T(1024)S(1)}, f32[8192]{0:T(1024)}, u32[]{:S(2)}) copy-start(f32[8192]{0:T(1024)} %param.7) | copy-start | bytes 98308
  87.0 25.8 %all-to-all-start.2 = ((bf16[4,4,128,128]{3,2,1,0:T(8,128)(2,1)}), bf16[4,4,128,128]{3,2,1,0:T(8,128)(2,1)S(1)}, u32[]{:S(2)}, u32[]{:S(2)}) async-start(bf16[4,4,128,128]{3,2,1,0:T(8,128)(2,1)} %get-tuple-element.29), calls=%async_computation.2 | async-start | bytes 1048576 | tf_op jit(solution)/shard_map/all_to_all | solution.py:345
  91.2 21.6 %collective-permute-start.6 = (bf16[4,128,128]{2,1,0:T(8,128)(2,1)S(1)}, bf16[4,128,128]{2,1,0:T(8,128)(2,1)S(1)}, u32[]{:S(2)}, u32[]{:S(2)}) collective-permute-start(bf16[4,128,128]{2,1,0:T(8,128)(2,1)S(1)} %get-tuple-element.34), channel_id=1, source_target_pairs={{0,256},{16,272},{32,288},{48,304},{64,320},{80,336},{96,352},{112... | collective-permute-start | bytes 393224 | tf_op jit(solution)/shard_map/ppermute | solution.py:340
  113.7 21.9 %all-to-all-start.4 = ((bf16[4,4,128,128]{3,2,1,0:T(8,128)(2,1)}), bf16[4,4,128,128]{3,2,1,0:T(8,128)(2,1)S(1)}, u32[]{:S(2)}, u32[]{:S(2)}) async-start(bf16[4,4,128,128]{3,2,1,0:T(8,128)(2,1)} %broadcast_in_dim.14), calls=%async_computation.4 | async-start | bytes 1048576 | tf_op jit(solution)/shard_map/all_to_all | solution.py:298
  118.5 17.1 %collective-permute-start.2 = (bf16[4,128,128]{2,1,0:T(8,128)(2,1)S(1)}, bf16[4,128,128]{2,1,0:T(8,128)(2,1)S(1)}, u32[]{:S(2)}, u32[]{:S(2)}) collective-permute-start(bf16[4,128,128]{2,1,0:T(8,128)(2,1)S(1)} %get-tuple-element.30), channel_id=1, source_target_pairs={{0,256},{16,272},{32,288},{48,304},{64,320},{80,336},{96,352},{112... | collective-permute-start | bytes 393224 | tf_op jit(solution)/shard_map/ppermute | solution.py:341
  136.5 33.3 %all-to-all-start.3 = ((bf16[4,4,128,128]{3,2,1,0:T(8,128)(2,1)}), bf16[4,4,128,128]{3,2,1,0:T(8,128)(2,1)S(1)}, u32[]{:S(2)}, u32[]{:S(2)}) async-start(bf16[4,4,128,128]{3,2,1,0:T(8,128)(2,1)} %broadcast_in_dim.13), calls=%async_computation.3 | async-start | bytes 1048576 | tf_op jit(solution)/shard_map/all_to_all | solution.py:298
  141.3 12.5 %collective-permute-start.3 = (bf16[8,128,128]{2,1,0:T(8,128)(2,1)S(1)}, bf16[8,128,128]{2,1,0:T(8,128)(2,1)S(1)}, u32[]{:S(2)}, u32[]{:S(2)}) collective-permute-start(bf16[8,128,128]{2,1,0:T(8,128)(2,1)S(1)} %get-tuple-element.31.k0_ref), channel_id=1, source_target_pairs={{0,64},{64,128},{128,192},{1,65},{65,129},{129,193},{2,66},{66,130... | collective-permute-start | bytes 786440 | tf_op jit(solution)/shard_map/ppermute | solution.py:344
  142.6 11.9 %collective-permute-start.4 = (bf16[8,128,128]{2,1,0:T(8,128)(2,1)S(1)}, bf16[8,128,128]{2,1,0:T(8,128)(2,1)S(1)}, u32[]{:S(2)}, u32[]{:S(2)}) collective-permute-start(bf16[8,128,128]{2,1,0:T(8,128)(2,1)S(1)} %get-tuple-element.31.k0_ref), channel_id=1, source_target_pairs={{0,128},{64,192},{1,129},{65,193},{2,130},{66,194},{3,131},{67,195... | collective-permute-start | bytes 786440 | tf_op jit(solution)/shard_map/ppermute | solution.py:344
  143.9 16.1 %collective-permute-start.5 = (bf16[8,128,128]{2,1,0:T(8,128)(2,1)S(1)}, bf16[8,128,128]{2,1,0:T(8,128)(2,1)S(1)}, u32[]{:S(2)}, u32[]{:S(2)}) collective-permute-start(bf16[8,128,128]{2,1,0:T(8,128)(2,1)S(1)} %get-tuple-element.31.k0_ref), channel_id=1, source_target_pairs={{0,192},{1,193},{2,194},{3,195},{4,196},{5,197},{6,198},{7,199},{8... | collective-permute-start | bytes 786440 | tf_op jit(solution)/shard_map/ppermute | solution.py:344
Sparse Core Ops, SparseCore 0:
  9.4 63.6 all-gather.2

commit v3 on v0

--- a/solution.py
+++ b/solution.py
@@ -30,6 +30,10 @@
     return pltpu.CompilerParams(vmem_limit_bytes=mib * 1024 * 1024)
 
 
+def line_at(i):
+    return 2 * i if i < 4 else 15 - 2 * i
+
+
 def scatter_kernel(row_ref, col_ref, live_ref, near_ref, there_ref, w_ref):
     def clear(i, c):
         w_ref[i] = jnp.zeros((HD, COLS * HD), jnp.bfloat16)
@@ -81,16 +85,17 @@
     acc_ref[...] = jnp.zeros_like(acc_ref)
 
     def step(i, c):
+        at = jnp.where(i < 4, 2 * i, 15 - 2 * i)
         part = None
         for ref, cc in ((mine_ref, core), (other_ref, 1 - core)):
-            x = ref[i].astype(jnp.float32) * r * gain_ref[2 * i + cc]
-            w = w_ref[pl.ds((2 * i + cc) * per, per)].reshape(chunk, COLS * HD)
+            x = ref[i].astype(jnp.float32) * r * gain_ref[2 * at + cc]
+            w = w_ref[pl.ds((2 * at + cc) * per, per)].reshape(chunk, COLS * HD)
             d = jnp.dot(x.astype(jnp.bfloat16), w, preferred_element_type=jnp.float32)
             part = d if part is None else part + d
         acc_ref[...] += part
         return c
 
-    lax.fori_loop(0, 8, step, 0)
+    lax.fori_loop(0, 8, step, 0, unroll=4)
     cosines = cos_ref[...]
     sines = sin_ref[...]
 
@@ -106,8 +111,9 @@
             qt = q[at].T.astype(jnp.bfloat16)
             for copy in range(4):
                 q_ref[copy, 2 * h + half] = qt
+            vt = v[at].T.astype(jnp.bfloat16)
             kv_ref[4 * h + half] = k[at]
-            kv_ref[4 * h + 2 + half] = v[at].T.astype(jnp.bfloat16)
+            kv_ref[4 * h + 2 + half] = vt
 
 
 def project(core, mine, other, w, gain, cosines, sines):
@@ -333,7 +339,9 @@
     core = lax.axis_index("core")
     plane = lax.axis_index(PLANE)
     block = zh * 16 + plane
-    mine = lax.all_gather(stream, "zl", axis=0, tiled=False)
+    mine = lax.all_gather(
+        stream, "zl", axis=0, tiled=False, axis_index_groups=[[line_at(i) for i in range(8)]]
+    )
     tv = tile_vals[0]
     there = lax.ppermute(tv, "zh", [(0, 1), (1, 0)])
     near_tiles = spread(tv, PLANE, 16).reshape(-1, HD, HD)
@@ -364,21 +372,22 @@
     other = lax.ppermute(mine, "core", [(0, 1), (1, 0)])
     w = scatter(rows, cols, live, near_tiles, there_tiles)
     q, kv = project(core.reshape(1), mine, other, w, gain, cosines, sines)
-    fars = []
-    for k in range(4):
-        pairs = [
-            (4 * y + x, 16 + 4 * ((y + k) % 4) + x) for y in range(4) for x in range(4)
-        ]
-        fars.append(lax.ppermute(kv, CTX, pairs))
+    across = [(b, 16 + b) for b in range(16)]
+    fars = [lax.ppermute(kv, CTX, across)]
     keys = [kv]
     for k in range(1, 4):
         keys.append(lax.ppermute(kv, "y", [(y, y + k) for y in range(4 - k)]))
     q = lax.all_to_all(q, "x", 0, 0, tiled=True)
+    for k in (1, 3, 2):
+        pairs = [
+            (16 + 4 * y + x, 16 + 4 * ((y + k) % 4) + x) for y in range(4) for x in range(4)
+        ]
+        fars.append(lax.ppermute(fars[0], CTX, pairs))
     ids = jnp.stack([zh, lax.axis_index("y"), lax.axis_index("x")]).astype(jnp.int32)
     acc, stat = near(ids, q, keys)
     acc, stat = far(ids, q, fars[:2], acc, stat)
-    parts = lax.all_to_all(last(ids, q, fars[2:], acc, stat), "x", 0, 0, tiled=True)
-    return combine(parts)
+    out = last(ids, q, fars[2:], acc, stat)
+    return combine(lax.all_to_all(out, "x", 0, 0, tiled=True))
 
 
 def solution(mesh):

time: 231 us -> 170 us (0.74)
  the two profiles are of different devices: /device:TPU:472 before, /device:TPU:448 now
where the time goes in v3:
time: 170 us; the launch traced here: 169 us
  waiting for transfers between devices  63.3 us (37%)
  starting transfers between devices  45.5 us (27%)
  Pallas kernels  26 us (15%)
  between operations  14.3 us (8%)
  blocking collectives  12.8 us (8%)
  local copies, waits for them, and re-layouts  5.04 us (3%)
  other arithmetic  2.08 us (1%)
    all_to_all x2, waiting for transfers between devices, spread(): return lax.all_to_all(many, axis, 0, 0, tiled=True)  21.1 us
    ppermute x1, waiting for transfers between devices, body(): fars = [lax.ppermute(kv, CTX, across)]  20.5 us
    ppermute x1, waiting for transfers between devices, body(): there = lax.ppermute(tv, 'zh', [(0, 1), (1, 0)])  16.2 us
    all_to_all x1, blocking collectives, body(): return combine(lax.all_to_all(out, 'x', 0, 0, tiled=True))  12.8 us
    all_to_all x2, starting transfers between devices, spread(): return lax.all_to_all(many, axis, 0, 0, tiled=True)  11.7 us
    ppermute x3, starting transfers between devices, body(): fars.append(lax.ppermute(fars[0], CTX, pairs))  11.2 us
    ppermute x3, starting transfers between devices, body(): keys.append(lax.ppermute(kv, 'y', [(y, y + k) for y in range(4 - k)]))  9.72 us
    pallas_call x1, Pallas kernels, project(): pl.pallas_call(project_kernel, out_shape=(jax.ShapeDtypeStruct((4, 4, HD,...  7.48 us
  transfers between devices with their start and end apart: 13, of which 6 were waited for; matrix products, arithmetic and copies ran while one was open for 4% of the time, Pallas kernels for 8%

profile of v3, /device:TPU:448, one launch (start us, length us, event | category | flops | bytes accessed | tf_op | source)
XLA Modules:
  0.0 169.0 jit_solution(16283234497807317488)
XLA Ops:
  6.5 0.7 all-gather.3.cloned.1.call-update
  7.3 2.4 %broadcast_in_dim.7 = bf16[16,3,128,128]{3,2,1,0:T(8,128)(2,1)} broadcast(bf16[3,128,128]{2,1,0:T(8,128)(2,1)} %bitcast.16), dimensions={1,2,3} | broadcast | bytes 1671168 | tf_op jit(solution)/shard_map/broadcast_in_dim | solution.py:333
  9.7 7.2 %all-to-all-start = ((bf16[16,3,128,128]{3,2,1,0:T(8,128)(2,1)}), bf16[16,3,128,128]{3,2,1,0:T(8,128)(2,1)S(1)}, u32[]{:S(2)}, u32[]{:S(2)}) async-start(bf16[16,3,128,128]{3,2,1,0:T(8,128)(2,1)} %broadcast_in_dim.7), calls=%async_computation | async-start | bytes 3145728 | tf_op jit(solution)/shard_map/all_to_all | solution.py:334
  16.9 5.4 %collective-permute-start = (bf16[3,128,128]{2,1,0:T(8,128)(2,1)S(1)}, bf16[3,128,128]{2,1,0:T(8,128)(2,1)S(1)}, u32[]{:S(2)}, u32[]{:S(2)}) collective-permute-start(bf16[3,128,128]{2,1,0:T(8,128)(2,1)S(1)} %bitcast.17), channel_id=1, source_target_pairs={{0,256},{256,0},{1,257},{257,1},{2,258},{258,2},{3,259},{259,3},{4... | collective-permute-start | bytes 294920 | tf_op jit(solution)/shard_map/ppermute | solution.py:346
  22.3 16.2 %collective-permute-done = bf16[3,128,128]{2,1,0:T(8,128)(2,1)S(1)} collective-permute-done((bf16[3,128,128]{2,1,0:T(8,128)(2,1)S(1)}, bf16[3,128,128]{2,1,0:T(8,128)(2,1)S(1)}, u32[]{:S(2)}, u32[]{:S(2)}) %collective-permute-start) | collective-permute-done | bytes 98336 | tf_op jit(solution)/shard_map/ppermute | solution.py:346
  38.5 2.9 %all-to-all-done = bf16[16,3,128,128]{3,2,1,0:T(8,128)(2,1)S(1)} async-done(((bf16[16,3,128,128]{3,2,1,0:T(8,128)(2,1)}), bf16[16,3,128,128]{3,2,1,0:T(8,128)(2,1)S(1)}, u32[]{:S(2)}, u32[]{:S(2)}) %all-to-all-start) | async-done | bytes 1572896 | tf_op jit(solution)/shard_map/all_to_all | solution.py:334
  41.4 1.5 broadcast_in_dim.8
  42.9 4.6 %all-to-all-start.1 = ((bf16[16,3,128,128]{3,2,1,0:T(8,128)(2,1)}), bf16[16,3,128,128]{3,2,1,0:T(8,128)(2,1)S(1)}, u32[]{:S(2)}, u32[]{:S(2)}) async-start(bf16[16,3,128,128]{3,2,1,0:T(8,128)(2,1)} %broadcast_in_dim.8), calls=%async_computation.1 | async-start | bytes 3145728 | tf_op jit(solution)/shard_map/all_to_all | solution.py:334
  47.5 0.6 broadcast.21
  48.1 0.6 reduce.7
  48.8 0.6 reduce.6
  50.6 0.5 fusion
  51.3 18.3 %all-to-all-done.1 = bf16[16,3,128,128]{3,2,1,0:T(8,128)(2,1)S(1)} async-done(((bf16[16,3,128,128]{3,2,1,0:T(8,128)(2,1)}), bf16[16,3,128,128]{3,2,1,0:T(8,128)(2,1)S(1)}, u32[]{:S(2)}, u32[]{:S(2)}) %all-to-all-start.1) | async-done | bytes 1572896 | tf_op jit(solution)/shard_map/all_to_all | solution.py:334
  69.5 3.5 %all-gather.3.cloned.1.call-done = bf16[2048,512]{1,0:T(8,128)(2,1)} async-done(((bf16[256,512]{1,0:T(8,128)(2,1)}), bf16[2048,512]{1,0:T(8,128)(2,1)}) %all-gather.3.cloned.1.call-update) | async-done | bytes 2097168 | tf_op jit(solution)/shard_map/all_gather | solution.py:342
  73.0 1.9 %collective-permute-start.1 = (bf16[8,256,512]{2,1,0:T(8,128)(2,1)}, bf16[8,256,512]{2,1,0:T(8,128)(2,1)}, u32[]{:S(2)}, u32[]{:S(2)}) collective-permute-start(bf16[8,256,512]{2,1,0:T(8,128)(2,1)} %bitcast.13), channel_id=1, source_target_pairs={{0,1},{1,0},{2,3},{3,2},{4,5},{5,4},{6,7},{7,6},{8,9},{9,8},{10,11... | collective-permute-start | bytes 6291464 | tf_op jit(solution)/shard_map/ppermute | solution.py:372
  74.9 3.1 %scatter_tiles.1.w_ref = bf16[64,128,768]{2,1,0:T(8,128)(2,1)S(1)} custom-call(s32[96]{0:T(128)S(1)} %reshape.48.row_ref, s32[96]{0:T(128)S(1)} %reshape.49.col_ref, s32[96]{0:T(128)S(1)} %reshape.54.live_ref, bf16[48,128,128]{2,1,0:T(8,128)(2,1)S(1)} %bitcast.11, bf16[48,128,128]{2,1,0:T(8,128)(2,1)S(1)} %bitcast.12), custom_call_target="tpu_custom_call" | custom-call | tf_op jit(solution)/shard_map/scatter_tiles/pallas_call | solution.py:60
  78.1 1.3 collective-permute-done.1.other_ref
  79.4 7.5 %project.1 = (bf16[4,4,128,128]{3,2,1,0:T(8,128)(2,1)}, bf16[8,128,128]{2,1,0:T(8,128)(2,1)S(1)}) custom-call(s32[1]{0:T(128)} %bitcast.3.core_ref, bf16[8,256,512]{2,1,0:T(8,128)(2,1)S(1)} %bitcast.14, bf16[8,256,512]{2,1,0:T(8,128)(2,1)} %collective-permute-done.1.other_ref, bf16[64,128,768]{2,1,0:T(8,128)(2,1)S(1)} %scatter_tiles.1.w_ref, ...), custom_call_target="tpu_custom_call" | custom-call | tf_op jit(solution)/shard_map/project/pallas_call | solution.py:120
  86.9 1.3 collective-permute-start.2
  88.2 3.8 %collective-permute-start.6 = (bf16[8,128,128]{2,1,0:T(8,128)(2,1)S(1)}, bf16[8,128,128]{2,1,0:T(8,128)(2,1)S(1)}, u32[]{:S(2)}, u32[]{:S(2)}) collective-permute-start(bf16[8,128,128]{2,1,0:T(8,128)(2,1)S(1)} %get-tuple-element.30.k0_ref), channel_id=1, source_target_pairs={{0,64},{64,128},{128,192},{1,65},{65,129},{129,193},{2,66},{66,130... | collective-permute-start | bytes 786440 | tf_op jit(solution)/shard_map/ppermute | solution.py:379
  92.0 4.3 %all-to-all-start.2 = ((bf16[4,4,128,128]{3,2,1,0:T(8,128)(2,1)}), bf16[4,4,128,128]{3,2,1,0:T(8,128)(2,1)S(1)}, u32[]{:S(2)}, u32[]{:S(2)}) async-start(bf16[4,4,128,128]{3,2,1,0:T(8,128)(2,1)} %get-tuple-element.29), calls=%async_computation.2 | async-start | bytes 1048576 | tf_op jit(solution)/shard_map/all_to_all | solution.py:380
  96.2 4.6 %collective-permute-start.7 = (bf16[8,128,128]{2,1,0:T(8,128)(2,1)S(1)}, bf16[8,128,128]{2,1,0:T(8,128)(2,1)S(1)}, u32[]{:S(2)}, u32[]{:S(2)}) collective-permute-start(bf16[8,128,128]{2,1,0:T(8,128)(2,1)S(1)} %get-tuple-element.30.k0_ref), channel_id=1, source_target_pairs={{0,128},{64,192},{1,129},{65,193},{2,130},{66,194},{3,131},{67,195... | collective-permute-start | bytes 786440 | tf_op jit(solution)/shard_map/ppermute | solution.py:379
  100.8 1.3 collective-permute-start.8
  102.2 20.5 %collective-permute-done.2.k0_ref = bf16[8,128,128]{2,1,0:T(8,128)(2,1)S(1)} collective-permute-done((bf16[8,128,128]{2,1,0:T(8,128)(2,1)S(1)}, bf16[8,128,128]{2,1,0:T(8,128)(2,1)S(1)}, u32[]{:S(2)}, u32[]{:S(2)}) %collective-permute-start.2) | collective-permute-done | bytes 262176 | tf_op jit(solution)/shard_map/ppermute | solution.py:376
  122.7 3.8 %collective-permute-start.5 = (bf16[8,128,128]{2,1,0:T(8,128)(2,1)S(1)}, bf16[8,128,128]{2,1,0:T(8,128)(2,1)S(1)}, u32[]{:S(2)}, u32[]{:S(2)}) collective-permute-start(bf16[8,128,128]{2,1,0:T(8,128)(2,1)S(1)} %collective-permute-done.2.k0_ref), channel_id=1, source_target_pairs={{256,320},{272,336},{288,352},{304,368},{320,384},{336,400},{352,4... | collective-permute-start | bytes 786440 | tf_op jit(solution)/shard_map/ppermute | solution.py:385
  126.4 3.3 %collective-permute-start.3 = (bf16[8,128,128]{2,1,0:T(8,128)(2,1)S(1)}, bf16[8,128,128]{2,1,0:T(8,128)(2,1)S(1)}, u32[]{:S(2)}, u32[]{:S(2)}) collective-permute-start(bf16[8,128,128]{2,1,0:T(8,128)(2,1)S(1)} %collective-permute-done.2.k0_ref), channel_id=1, source_target_pairs={{256,448},{272,464},{288,480},{304,496},{320,256},{336,272},{352,2... | collective-permute-start | bytes 786440 | tf_op jit(solution)/shard_map/ppermute | solution.py:385
  129.7 4.1 %collective-permute-start.4 = (bf16[8,128,128]{2,1,0:T(8,128)(2,1)S(1)}, bf16[8,128,128]{2,1,0:T(8,128)(2,1)S(1)}, u32[]{:S(2)}, u32[]{:S(2)}) collective-permute-start(bf16[8,128,128]{2,1,0:T(8,128)(2,1)S(1)} %collective-permute-done.2.k0_ref), channel_id=1, source_target_pairs={{256,384},{272,400},{288,416},{304,432},{320,448},{336,464},{352,4... | collective-permute-start | bytes 786440 | tf_op jit(solution)/shard_map/ppermute | solution.py:385
  133.9 6.5 %attend_near.1 = (f32[8,128,256]{2,1,0:T(8,128)S(1)}, f32[8,8,256]{2,1,0:T(8,128)S(1)}) custom-call(s32[3]{0:T(128)S(1)} %pad_add_fusion.ids_ref, bf16[4,4,128,128]{3,2,1,0:T(8,128)(2,1)S(1)} %all-to-all-done.2.q_ref, bf16[8,128,128]{2,1,0:T(8,128)(2,1)S(1)} %get-tuple-element.30.k0_ref, bf16[8,128,128]{2,1,0:T(8,128)(2,1)S(1)} %collective-permute-done.6.k1_ref, ...), custom_call_target="tpu_custom_call" | custom-call | tf_op jit(solution)/shard_map/attend_near/pallas_call | solution.py:192
  140.5 4.0 %attend_far.1 = (f32[8,128,256]{2,1,0:T(8,128)S(1)}, f32[8,8,256]{2,1,0:T(8,128)S(1)}) custom-call(s32[3]{0:T(128)S(1)} %pad_add_fusion.ids_ref, bf16[4,4,128,128]{3,2,1,0:T(8,128)(2,1)S(1)} %all-to-all-done.2.q_ref, bf16[8,128,128]{2,1,0:T(8,128)(2,1)S(1)} %collective-permute-done.2.k0_ref, bf16[8,128,128]{2,1,0:T(8,128)(2,1)S(1)} %collective-permute-done.5.k1_ref, ...), custom_call_target="tpu_custom_call" | custom-call | tf_op jit(solution)/shard_map/attend_far/pallas_call | solution.py:244
  144.5 4.0 %attend_last.1 = bf16[4,144,512]{2,1,0:T(8,128)(2,1)S(1)} custom-call(s32[3]{0:T(128)S(1)} %pad_add_fusion.ids_ref, bf16[4,4,128,128]{3,2,1,0:T(8,128)(2,1)S(1)} %all-to-all-done.2.q_ref, bf16[8,128,128]{2,1,0:T(8,128)(2,1)S(1)} %collective-permute-done.3.k0_ref, bf16[8,128,128]{2,1,0:T(8,128)(2,1)S(1)} %collective-permute-done.4.k1_ref, ...), custom_call_target="tpu_custom_call" | custom-call | tf_op jit(solution)/shard_map/attend_last/pallas_call | solution.py:294
  148.5 12.8 %all_to_all.20.parts_ref = bf16[4,144,512]{2,1,0:T(8,128)(2,1)S(1)} all-to-all(bf16[4,144,512]{2,1,0:T(8,128)(2,1)S(1)} %attend_last.1), channel_id=1, replica_groups=mesh['zh'=2,'y'=4,'x'=4,'zl'=8,'core'=2] {'x'}, dimensions={0} | all-to-all | bytes 1179648 | tf_op jit(solution)/shard_map/all_to_all | solution.py:390
  161.3 0.9 combine.1
  (33 shorter events, 0.8 us)
Async XLA Ops:
  6.5 66.5 %all-gather.3.cloned.1.call-start = ((), (), s32[]{:S(2)}) async-start(), calls=%async_computation.4 | async-start | bytes 2359296 | tf_op jit(solution)/shard_map/all_gather | solution.py:342
  9.7 7.2 %copy-start.2 = (bf16[1,3,128,128]{3,2,1,0:T(8,128)(2,1)S(1)}, bf16[1,3,128,128]{3,2,1,0:T(8,128)(2,1)}, u32[]{:S(2)}) copy-start(bf16[1,3,128,128]{3,2,1,0:T(8,128)(2,1)} %param.8) | copy-start | bytes 294916
  9.7 31.7 %all-to-all-start = ((bf16[16,3,128,128]{3,2,1,0:T(8,128)(2,1)}), bf16[16,3,128,128]{3,2,1,0:T(8,128)(2,1)S(1)}, u32[]{:S(2)}, u32[]{:S(2)}) async-start(bf16[16,3,128,128]{3,2,1,0:T(8,128)(2,1)} %broadcast_in_dim.7), calls=%async_computation | async-start | bytes 3145728 | tf_op jit(solution)/shard_map/all_to_all | solution.py:334
  16.9 21.6 %collective-permute-start = (bf16[3,128,128]{2,1,0:T(8,128)(2,1)S(1)}, bf16[3,128,128]{2,1,0:T(8,128)(2,1)S(1)}, u32[]{:S(2)}, u32[]{:S(2)}) collective-permute-start(bf16[3,128,128]{2,1,0:T(8,128)(2,1)S(1)} %bitcast.17), channel_id=1, source_target_pairs={{0,256},{256,0},{1,257},{257,1},{2,258},{258,2},{3,259},{259,3},{4... | collective-permute-start | bytes 294920 | tf_op jit(solution)/shard_map/ppermute | solution.py:346
  42.9 5.2 %copy-start.3 = (s32[1,96]{1,0:T(1,128)S(1)}, s32[1,96]{1,0:T(1,128)}, u32[]{:S(2)}) copy-start(s32[1,96]{1,0:T(1,128)} %param.10) | copy-start | bytes 1156
  42.9 5.9 %copy-start.4 = (s32[1,96]{1,0:T(1,128)S(1)}, s32[1,96]{1,0:T(1,128)}, u32[]{:S(2)}) copy-start(s32[1,96]{1,0:T(1,128)} %param.9) | copy-start | bytes 1156
  42.9 26.6 %all-to-all-start.1 = ((bf16[16,3,128,128]{3,2,1,0:T(8,128)(2,1)}), bf16[16,3,128,128]{3,2,1,0:T(8,128)(2,1)S(1)}, u32[]{:S(2)}, u32[]{:S(2)}) async-start(bf16[16,3,128,128]{3,2,1,0:T(8,128)(2,1)} %broadcast_in_dim.8), calls=%async_computation.1 | async-start | bytes 3145728 | tf_op jit(solution)/shard_map/all_to_all | solution.py:334
  73.0 6.4 %collective-permute-start.1 = (bf16[8,256,512]{2,1,0:T(8,128)(2,1)}, bf16[8,256,512]{2,1,0:T(8,128)(2,1)}, u32[]{:S(2)}, u32[]{:S(2)}) collective-permute-start(bf16[8,256,512]{2,1,0:T(8,128)(2,1)} %bitcast.13), channel_id=1, source_target_pairs={{0,1},{1,0},{2,3},{3,2},{4,5},{5,4},{6,7},{7,6},{8,9},{9,8},{10,11... | collective-permute-start | bytes 6291464 | tf_op jit(solution)/shard_map/ppermute | solution.py:372
  74.9 4.5 %copy-start = (bf16[2048,512]{1,0:T(8,128)(2,1)S(1)}, bf16[2048,512]{1,0:T(8,128)(2,1)}, u32[]{:S(2)}) copy-start(bf16[2048,512]{1,0:T(8,128)(2,1)} %all-gather.3.cloned.1.call-done) | copy-start | bytes 6291460
  74.9 4.5 %copy-start.1 = (f32[8192]{0:T(1024)S(1)}, f32[8192]{0:T(1024)}, u32[]{:S(2)}) copy-start(f32[8192]{0:T(1024)} %param.7) | copy-start | bytes 98308
  86.9 35.8 %collective-permute-start.2 = (bf16[8,128,128]{2,1,0:T(8,128)(2,1)S(1)}, bf16[8,128,128]{2,1,0:T(8,128)(2,1)S(1)}, u32[]{:S(2)}, u32[]{:S(2)}) collective-permute-start(bf16[8,128,128]{2,1,0:T(8,128)(2,1)S(1)} %get-tuple-element.30.k0_ref), channel_id=1, source_target_pairs={{0,256},{16,272},{32,288},{48,304},{64,320},{80,336},{96,352},{112... | collective-permute-start | bytes 786440 | tf_op jit(solution)/shard_map/ppermute | solution.py:376
  88.2 41.6 %collective-permute-start.6 = (bf16[8,128,128]{2,1,0:T(8,128)(2,1)S(1)}, bf16[8,128,128]{2,1,0:T(8,128)(2,1)S(1)}, u32[]{:S(2)}, u32[]{:S(2)}) collective-permute-start(bf16[8,128,128]{2,1,0:T(8,128)(2,1)S(1)} %get-tuple-element.30.k0_ref), channel_id=1, source_target_pairs={{0,64},{64,128},{128,192},{1,65},{65,129},{129,193},{2,66},{66,130... | collective-permute-start | bytes 786440 | tf_op jit(solution)/shard_map/ppermute | solution.py:379
  92.0 42.0 %all-to-all-start.2 = ((bf16[4,4,128,128]{3,2,1,0:T(8,128)(2,1)}), bf16[4,4,128,128]{3,2,1,0:T(8,128)(2,1)S(1)}, u32[]{:S(2)}, u32[]{:S(2)}) async-start(bf16[4,4,128,128]{3,2,1,0:T(8,128)(2,1)} %get-tuple-element.29), calls=%async_computation.2 | async-start | bytes 1048576 | tf_op jit(solution)/shard_map/all_to_all | solution.py:380
  96.2 37.7 %collective-permute-start.7 = (bf16[8,128,128]{2,1,0:T(8,128)(2,1)S(1)}, bf16[8,128,128]{2,1,0:T(8,128)(2,1)S(1)}, u32[]{:S(2)}, u32[]{:S(2)}) collective-permute-start(bf16[8,128,128]{2,1,0:T(8,128)(2,1)S(1)} %get-tuple-element.30.k0_ref), channel_id=1, source_target_pairs={{0,128},{64,192},{1,129},{65,193},{2,130},{66,194},{3,131},{67,195... | collective-permute-start | bytes 786440 | tf_op jit(solution)/shard_map/ppermute | solution.py:379
  100.8 33.1 %collective-permute-start.8 = (bf16[8,128,128]{2,1,0:T(8,128)(2,1)S(1)}, bf16[8,128,128]{2,1,0:T(8,128)(2,1)S(1)}, u32[]{:S(2)}, u32[]{:S(2)}) collective-permute-start(bf16[8,128,128]{2,1,0:T(8,128)(2,1)S(1)} %get-tuple-element.30.k0_ref), channel_id=1, source_target_pairs={{0,192},{1,193},{2,194},{3,195},{4,196},{5,197},{6,198},{7,199},{8... | collective-permute-start | bytes 786440 | tf_op jit(solution)/shard_map/ppermute | solution.py:379
  122.7 17.8 %collective-permute-start.5 = (bf16[8,128,128]{2,1,0:T(8,128)(2,1)S(1)}, bf16[8,128,128]{2,1,0:T(8,128)(2,1)S(1)}, u32[]{:S(2)}, u32[]{:S(2)}) collective-permute-start(bf16[8,128,128]{2,1,0:T(8,128)(2,1)S(1)} %collective-permute-done.2.k0_ref), channel_id=1, source_target_pairs={{256,320},{272,336},{288,352},{304,368},{320,384},{336,400},{352,4... | collective-permute-start | bytes 786440 | tf_op jit(solution)/shard_map/ppermute | solution.py:385
  126.4 18.0 %collective-permute-start.3 = (bf16[8,128,128]{2,1,0:T(8,128)(2,1)S(1)}, bf16[8,128,128]{2,1,0:T(8,128)(2,1)S(1)}, u32[]{:S(2)}, u32[]{:S(2)}) collective-permute-start(bf16[8,128,128]{2,1,0:T(8,128)(2,1)S(1)} %collective-permute-done.2.k0_ref), channel_id=1, source_target_pairs={{256,448},{272,464},{288,480},{304,496},{320,256},{336,272},{352,2... | collective-permute-start | bytes 786440 | tf_op jit(solution)/shard_map/ppermute | solution.py:385
  129.7 14.8 %collective-permute-start.4 = (bf16[8,128,128]{2,1,0:T(8,128)(2,1)S(1)}, bf16[8,128,128]{2,1,0:T(8,128)(2,1)S(1)}, u32[]{:S(2)}, u32[]{:S(2)}) collective-permute-start(bf16[8,128,128]{2,1,0:T(8,128)(2,1)S(1)} %collective-permute-done.2.k0_ref), channel_id=1, source_target_pairs={{256,384},{272,400},{288,416},{304,432},{320,448},{336,464},{352,4... | collective-permute-start | bytes 786440 | tf_op jit(solution)/shard_map/ppermute | solution.py:385
Sparse Core Ops, SparseCore 0:
  9.4 63.5 all-gather.2

commit v4 on v3

--- a/solution.py
+++ b/solution.py
@@ -95,7 +95,7 @@
         acc_ref[...] += part
         return c
 
-    lax.fori_loop(0, 8, step, 0, unroll=4)
+    lax.fori_loop(0, 8, step, 0, unroll=8)
     cosines = cos_ref[...]
     sines = sin_ref[...]
 
@@ -103,7 +103,7 @@
         return v * cosines + pltpu.roll(v, HD // 2, 1) * sines
 
     for h in range(2):
-        q = rot(acc_ref[:, h * HD:(h + 1) * HD])
+        q = rot(acc_ref[:, h * HD:(h + 1) * HD]) * SCALE
         k = rot(acc_ref[:, (2 + h) * HD:(3 + h) * HD]).astype(jnp.bfloat16)
         v = acc_ref[:, (4 + h) * HD:(5 + h) * HD]
         for half in range(2):
@@ -167,7 +167,7 @@
             acc = None
             total = None
             for ref, kid, s in zip(refs, kids, ss):
-                p = jnp.where(gap <= (qid - kid) * TOK, jnp.exp2((s - top) * SCALE), 0.0)
+                p = jnp.where(gap <= (qid - kid) * TOK, jnp.exp2(s - top), 0.0)
                 t = jnp.sum(p, axis=0, keepdims=True)
                 o = jnp.dot(
                     load_v(ref, h), p.astype(jnp.bfloat16), preferred_element_type=jnp.float32
@@ -179,7 +179,7 @@
             stat_ref[2 * n + h, 1:2] = total
         return c
 
-    lax.fori_loop(0, 4, one_source, 0)
+    lax.fori_loop(0, 4, one_source, 0, unroll=2)
 
 
 STATE = (
@@ -203,11 +203,11 @@
     q = load_q(q_ref, n, h)
     ss = [jnp.dot(load_k(ref, h), q, preferred_element_type=jnp.float32) for ref in refs]
     top = functools.reduce(jnp.maximum, [jnp.max(s, axis=0, keepdims=True) for s in ss], old)
-    fac = jnp.exp2((old - top) * SCALE)
+    fac = jnp.exp2(old - top)
     acc = acc * fac
     total = total * fac
     for s, ref in zip(ss, refs):
-        p = jnp.exp2((s - top) * SCALE)
+        p = jnp.exp2(s - top)
         total = total + jnp.sum(p, axis=0, keepdims=True)
         acc = acc + jnp.dot(
             load_v(ref, h), p.astype(jnp.bfloat16), preferred_element_type=jnp.float32
@@ -232,7 +232,7 @@
 
     @pl.when(late)
     def _():
-        lax.fori_loop(0, 4, one_source, 0)
+        lax.fori_loop(0, 4, one_source, 0, unroll=2)
 
     @pl.when(jnp.logical_not(late))
     def _():
@@ -257,7 +257,7 @@
     def finish(n, h, acc, top, total):
         some = total > 0
         safe = jnp.where(some, total, 1.0)
-        lse = jnp.where(some, top * SCALE + jnp.log2(safe), NEG)
+        lse = jnp.where(some, top + jnp.log2(safe), NEG)
         at = slice(h * TOK, (h + 1) * TOK)
         out_ref[n, 0:HD, at] = (acc / safe).astype(jnp.bfloat16)
         hi = lse.astype(jnp.bfloat16).astype(jnp.float32)
@@ -278,7 +278,7 @@
                 finish(n, h, *state(n, h))
             return c
 
-        lax.fori_loop(0, 4, one_source, 0)
+        lax.fori_loop(0, 4, one_source, 0, unroll=2)
 
     @pl.when(late)
     def _():
@@ -287,7 +287,7 @@
                 finish(n, h, *fold(q_ref, (k0_ref, k1_ref), n, h, *state(n, h)))
             return c
 
-        lax.fori_loop(0, 4, one_source, 0)
+        lax.fori_loop(0, 4, one_source, 0, unroll=2)
 
 
 def last(ids, q, fars, acc, stat):

time: 170 us -> 167 us (0.982)
  Pallas kernels: 26 us -> 23.7 us
  transfers between devices with their start and end apart: 13 -> 13, of which waited for: 6 -> 6; matrix products, arithmetic and copies ran while one was open for 4% -> 4% of each run, Pallas kernels for 8% -> 7%
where the time goes in v4:
time: 167 us
  waiting for transfers between devices  63.3 us (38%)
  starting transfers between devices  45.5 us (27%)
  Pallas kernels  23.7 us (14%)
  between operations  14.3 us (9%)
  blocking collectives  12.8 us (8%)
  local copies, waits for them, and re-layouts  5.04 us (3%)
  other arithmetic  2.08 us (1%)
    all_to_all x2, waiting for transfers between devices, spread(): return lax.all_to_all(many, axis, 0, 0, tiled=True)  21.1 us
    ppermute x1, waiting for transfers between devices, body(): fars = [lax.ppermute(kv, CTX, across)]  20.5 us
    ppermute x1, waiting for transfers between devices, body(): there = lax.ppermute(tv, 'zh', [(0, 1), (1, 0)])  16.2 us
    all_to_all x1, blocking collectives, body(): return combine(lax.all_to_all(out, 'x', 0, 0, tiled=True))  12.8 us
    all_to_all x2, starting transfers between devices, spread(): return lax.all_to_all(many, axis, 0, 0, tiled=True)  11.7 us
    ppermute x3, starting transfers between devices, body(): fars.append(lax.ppermute(fars[0], CTX, pairs))  11.2 us
    ppermute x3, starting transfers between devices, body(): keys.append(lax.ppermute(kv, 'y', [(y, y + k) for y in range(4 - k)]))  9.75 us
    pallas_call x1, Pallas kernels, project(): pl.pallas_call(project_kernel, out_shape=(jax.ShapeDtypeStruct((4, 4, HD,...  7.12 us
  transfers between devices with their start and end apart: 13, of which 6 were waited for; matrix products, arithmetic and copies ran while one was open for 4% of the time, Pallas kernels for 7%

profile of v4, /device:TPU:448, one launch (start us, length us, event | category | flops | bytes accessed | tf_op | source)
XLA Modules:
  0.0 166.8 jit_solution(6454404362854303899)
XLA Ops:
  6.5 0.7 all-gather.3.cloned.1.call-update
  7.3 2.4 %broadcast_in_dim.7 = bf16[16,3,128,128]{3,2,1,0:T(8,128)(2,1)} broadcast(bf16[3,128,128]{2,1,0:T(8,128)(2,1)} %bitcast.16), dimensions={1,2,3} | broadcast | bytes 1671168 | tf_op jit(solution)/shard_map/broadcast_in_dim | solution.py:333
  9.7 7.2 %all-to-all-start = ((bf16[16,3,128,128]{3,2,1,0:T(8,128)(2,1)}), bf16[16,3,128,128]{3,2,1,0:T(8,128)(2,1)S(1)}, u32[]{:S(2)}, u32[]{:S(2)}) async-start(bf16[16,3,128,128]{3,2,1,0:T(8,128)(2,1)} %broadcast_in_dim.7), calls=%async_computation | async-start | bytes 3145728 | tf_op jit(solution)/shard_map/all_to_all | solution.py:334
  16.9 5.4 %collective-permute-start = (bf16[3,128,128]{2,1,0:T(8,128)(2,1)S(1)}, bf16[3,128,128]{2,1,0:T(8,128)(2,1)S(1)}, u32[]{:S(2)}, u32[]{:S(2)}) collective-permute-start(bf16[3,128,128]{2,1,0:T(8,128)(2,1)S(1)} %bitcast.17), channel_id=1, source_target_pairs={{0,256},{256,0},{1,257},{257,1},{2,258},{258,2},{3,259},{259,3},{4... | collective-permute-start | bytes 294920 | tf_op jit(solution)/shard_map/ppermute | solution.py:346
  22.3 16.2 %collective-permute-done = bf16[3,128,128]{2,1,0:T(8,128)(2,1)S(1)} collective-permute-done((bf16[3,128,128]{2,1,0:T(8,128)(2,1)S(1)}, bf16[3,128,128]{2,1,0:T(8,128)(2,1)S(1)}, u32[]{:S(2)}, u32[]{:S(2)}) %collective-permute-start) | collective-permute-done | bytes 98336 | tf_op jit(solution)/shard_map/ppermute | solution.py:346
  38.5 2.9 %all-to-all-done = bf16[16,3,128,128]{3,2,1,0:T(8,128)(2,1)S(1)} async-done(((bf16[16,3,128,128]{3,2,1,0:T(8,128)(2,1)}), bf16[16,3,128,128]{3,2,1,0:T(8,128)(2,1)S(1)}, u32[]{:S(2)}, u32[]{:S(2)}) %all-to-all-start) | async-done | bytes 1572896 | tf_op jit(solution)/shard_map/all_to_all | solution.py:334
  41.4 1.5 broadcast_in_dim.8
  42.9 4.6 %all-to-all-start.1 = ((bf16[16,3,128,128]{3,2,1,0:T(8,128)(2,1)}), bf16[16,3,128,128]{3,2,1,0:T(8,128)(2,1)S(1)}, u32[]{:S(2)}, u32[]{:S(2)}) async-start(bf16[16,3,128,128]{3,2,1,0:T(8,128)(2,1)} %broadcast_in_dim.8), calls=%async_computation.1 | async-start | bytes 3145728 | tf_op jit(solution)/shard_map/all_to_all | solution.py:334
  47.5 0.6 broadcast.21
  48.1 0.6 reduce.7
  48.8 0.6 reduce.6
  50.6 0.5 fusion
  51.3 18.3 %all-to-all-done.1 = bf16[16,3,128,128]{3,2,1,0:T(8,128)(2,1)S(1)} async-done(((bf16[16,3,128,128]{3,2,1,0:T(8,128)(2,1)}), bf16[16,3,128,128]{3,2,1,0:T(8,128)(2,1)S(1)}, u32[]{:S(2)}, u32[]{:S(2)}) %all-to-all-start.1) | async-done | bytes 1572896 | tf_op jit(solution)/shard_map/all_to_all | solution.py:334
  69.5 3.5 %all-gather.3.cloned.1.call-done = bf16[2048,512]{1,0:T(8,128)(2,1)} async-done(((bf16[256,512]{1,0:T(8,128)(2,1)}), bf16[2048,512]{1,0:T(8,128)(2,1)}) %all-gather.3.cloned.1.call-update) | async-done | bytes 2097168 | tf_op jit(solution)/shard_map/all_gather | solution.py:342
  73.0 1.9 %collective-permute-start.1 = (bf16[8,256,512]{2,1,0:T(8,128)(2,1)}, bf16[8,256,512]{2,1,0:T(8,128)(2,1)}, u32[]{:S(2)}, u32[]{:S(2)}) collective-permute-start(bf16[8,256,512]{2,1,0:T(8,128)(2,1)} %bitcast.13), channel_id=1, source_target_pairs={{0,1},{1,0},{2,3},{3,2},{4,5},{5,4},{6,7},{7,6},{8,9},{9,8},{10,11... | collective-permute-start | bytes 6291464 | tf_op jit(solution)/shard_map/ppermute | solution.py:372
  74.9 3.1 %scatter_tiles.1.w_ref = bf16[64,128,768]{2,1,0:T(8,128)(2,1)S(1)} custom-call(s32[96]{0:T(128)S(1)} %reshape.48.row_ref, s32[96]{0:T(128)S(1)} %reshape.49.col_ref, s32[96]{0:T(128)S(1)} %reshape.54.live_ref, bf16[48,128,128]{2,1,0:T(8,128)(2,1)S(1)} %bitcast.11, bf16[48,128,128]{2,1,0:T(8,128)(2,1)S(1)} %bitcast.12), custom_call_target="tpu_custom_call" | custom-call | tf_op jit(solution)/shard_map/scatter_tiles/pallas_call | solution.py:60
  78.1 1.3 collective-permute-done.1.other_ref
  79.4 7.1 %project.1 = (bf16[4,4,128,128]{3,2,1,0:T(8,128)(2,1)}, bf16[8,128,128]{2,1,0:T(8,128)(2,1)S(1)}) custom-call(s32[1]{0:T(128)} %bitcast.3.core_ref, bf16[8,256,512]{2,1,0:T(8,128)(2,1)S(1)} %bitcast.14, bf16[8,256,512]{2,1,0:T(8,128)(2,1)} %collective-permute-done.1.other_ref, bf16[64,128,768]{2,1,0:T(8,128)(2,1)S(1)} %scatter_tiles.1.w_ref, ...), custom_call_target="tpu_custom_call" | custom-call | tf_op jit(solution)/shard_map/project/pallas_call | solution.py:120
  86.5 1.3 collective-permute-start.2
  87.8 3.8 %collective-permute-start.6 = (bf16[8,128,128]{2,1,0:T(8,128)(2,1)S(1)}, bf16[8,128,128]{2,1,0:T(8,128)(2,1)S(1)}, u32[]{:S(2)}, u32[]{:S(2)}) collective-permute-start(bf16[8,128,128]{2,1,0:T(8,128)(2,1)S(1)} %get-tuple-element.30.k0_ref), channel_id=1, source_target_pairs={{0,64},{64,128},{128,192},{1,65},{65,129},{129,193},{2,66},{66,130... | collective-permute-start | bytes 786440 | tf_op jit(solution)/shard_map/ppermute | solution.py:379
  91.6 4.3 %all-to-all-start.2 = ((bf16[4,4,128,128]{3,2,1,0:T(8,128)(2,1)}), bf16[4,4,128,128]{3,2,1,0:T(8,128)(2,1)S(1)}, u32[]{:S(2)}, u32[]{:S(2)}) async-start(bf16[4,4,128,128]{3,2,1,0:T(8,128)(2,1)} %get-tuple-element.29), calls=%async_computation.2 | async-start | bytes 1048576 | tf_op jit(solution)/shard_map/all_to_all | solution.py:380
  95.9 4.6 %collective-permute-start.7 = (bf16[8,128,128]{2,1,0:T(8,128)(2,1)S(1)}, bf16[8,128,128]{2,1,0:T(8,128)(2,1)S(1)}, u32[]{:S(2)}, u32[]{:S(2)}) collective-permute-start(bf16[8,128,128]{2,1,0:T(8,128)(2,1)S(1)} %get-tuple-element.30.k0_ref), channel_id=1, source_target_pairs={{0,128},{64,192},{1,129},{65,193},{2,130},{66,194},{3,131},{67,195... | collective-permute-start | bytes 786440 | tf_op jit(solution)/shard_map/ppermute | solution.py:379
  100.5 1.3 collective-permute-start.8
  101.8 20.5 %collective-permute-done.2.k0_ref = bf16[8,128,128]{2,1,0:T(8,128)(2,1)S(1)} collective-permute-done((bf16[8,128,128]{2,1,0:T(8,128)(2,1)S(1)}, bf16[8,128,128]{2,1,0:T(8,128)(2,1)S(1)}, u32[]{:S(2)}, u32[]{:S(2)}) %collective-permute-start.2) | collective-permute-done | bytes 262176 | tf_op jit(solution)/shard_map/ppermute | solution.py:376
  122.3 3.8 %collective-permute-start.5 = (bf16[8,128,128]{2,1,0:T(8,128)(2,1)S(1)}, bf16[8,128,128]{2,1,0:T(8,128)(2,1)S(1)}, u32[]{:S(2)}, u32[]{:S(2)}) collective-permute-start(bf16[8,128,128]{2,1,0:T(8,128)(2,1)S(1)} %collective-permute-done.2.k0_ref), channel_id=1, source_target_pairs={{256,320},{272,336},{288,352},{304,368},{320,384},{336,400},{352,4... | collective-permute-start | bytes 786440 | tf_op jit(solution)/shard_map/ppermute | solution.py:385
  126.1 3.2 %collective-permute-start.3 = (bf16[8,128,128]{2,1,0:T(8,128)(2,1)S(1)}, bf16[8,128,128]{2,1,0:T(8,128)(2,1)S(1)}, u32[]{:S(2)}, u32[]{:S(2)}) collective-permute-start(bf16[8,128,128]{2,1,0:T(8,128)(2,1)S(1)} %collective-permute-done.2.k0_ref), channel_id=1, source_target_pairs={{256,448},{272,464},{288,480},{304,496},{320,256},{336,272},{352,2... | collective-permute-start | bytes 786440 | tf_op jit(solution)/shard_map/ppermute | solution.py:385
  129.4 4.1 %collective-permute-start.4 = (bf16[8,128,128]{2,1,0:T(8,128)(2,1)S(1)}, bf16[8,128,128]{2,1,0:T(8,128)(2,1)S(1)}, u32[]{:S(2)}, u32[]{:S(2)}) collective-permute-start(bf16[8,128,128]{2,1,0:T(8,128)(2,1)S(1)} %collective-permute-done.2.k0_ref), channel_id=1, source_target_pairs={{256,384},{272,400},{288,416},{304,432},{320,448},{336,464},{352,4... | collective-permute-start | bytes 786440 | tf_op jit(solution)/shard_map/ppermute | solution.py:385
  133.6 5.7 %attend_near.1 = (f32[8,128,256]{2,1,0:T(8,128)S(1)}, f32[8,8,256]{2,1,0:T(8,128)S(1)}) custom-call(s32[3]{0:T(128)S(1)} %pad_add_fusion.ids_ref, bf16[4,4,128,128]{3,2,1,0:T(8,128)(2,1)S(1)} %all-to-all-done.2.q_ref, bf16[8,128,128]{2,1,0:T(8,128)(2,1)S(1)} %get-tuple-element.30.k0_ref, bf16[8,128,128]{2,1,0:T(8,128)(2,1)S(1)} %collective-permute-done.6.k1_ref, ...), custom_call_target="tpu_custom_call" | custom-call | tf_op jit(solution)/shard_map/attend_near/pallas_call | solution.py:192
  139.3 3.4 %attend_far.1 = (f32[8,128,256]{2,1,0:T(8,128)S(1)}, f32[8,8,256]{2,1,0:T(8,128)S(1)}) custom-call(s32[3]{0:T(128)S(1)} %pad_add_fusion.ids_ref, bf16[4,4,128,128]{3,2,1,0:T(8,128)(2,1)S(1)} %all-to-all-done.2.q_ref, bf16[8,128,128]{2,1,0:T(8,128)(2,1)S(1)} %collective-permute-done.2.k0_ref, bf16[8,128,128]{2,1,0:T(8,128)(2,1)S(1)} %collective-permute-done.5.k1_ref, ...), custom_call_target="tpu_custom_call" | custom-call | tf_op jit(solution)/shard_map/attend_far/pallas_call | solution.py:244
  142.7 3.5 %attend_last.1 = bf16[4,144,512]{2,1,0:T(8,128)(2,1)S(1)} custom-call(s32[3]{0:T(128)S(1)} %pad_add_fusion.ids_ref, bf16[4,4,128,128]{3,2,1,0:T(8,128)(2,1)S(1)} %all-to-all-done.2.q_ref, bf16[8,128,128]{2,1,0:T(8,128)(2,1)S(1)} %collective-permute-done.3.k0_ref, bf16[8,128,128]{2,1,0:T(8,128)(2,1)S(1)} %collective-permute-done.4.k1_ref, ...), custom_call_target="tpu_custom_call" | custom-call | tf_op jit(solution)/shard_map/attend_last/pallas_call | solution.py:294
  146.2 12.8 %all_to_all.20.parts_ref = bf16[4,144,512]{2,1,0:T(8,128)(2,1)S(1)} all-to-all(bf16[4,144,512]{2,1,0:T(8,128)(2,1)S(1)} %attend_last.1), channel_id=1, replica_groups=mesh['zh'=2,'y'=4,'x'=4,'zl'=8,'core'=2] {'x'}, dimensions={0} | all-to-all | bytes 1179648 | tf_op jit(solution)/shard_map/all_to_all | solution.py:390
  159.1 0.9 combine.1
  (33 shorter events, 0.8 us)
Async XLA Ops:
  6.5 66.5 %all-gather.3.cloned.1.call-start = ((), (), s32[]{:S(2)}) async-start(), calls=%async_computation.4 | async-start | bytes 2359296 | tf_op jit(solution)/shard_map/all_gather | solution.py:342
  9.7 7.2 %copy-start.2 = (bf16[1,3,128,128]{3,2,1,0:T(8,128)(2,1)S(1)}, bf16[1,3,128,128]{3,2,1,0:T(8,128)(2,1)}, u32[]{:S(2)}) copy-start(bf16[1,3,128,128]{3,2,1,0:T(8,128)(2,1)} %param.8) | copy-start | bytes 294916
  9.7 31.7 %all-to-all-start = ((bf16[16,3,128,128]{3,2,1,0:T(8,128)(2,1)}), bf16[16,3,128,128]{3,2,1,0:T(8,128)(2,1)S(1)}, u32[]{:S(2)}, u32[]{:S(2)}) async-start(bf16[16,3,128,128]{3,2,1,0:T(8,128)(2,1)} %broadcast_in_dim.7), calls=%async_computation | async-start | bytes 3145728 | tf_op jit(solution)/shard_map/all_to_all | solution.py:334
  16.9 21.6 %collective-permute-start = (bf16[3,128,128]{2,1,0:T(8,128)(2,1)S(1)}, bf16[3,128,128]{2,1,0:T(8,128)(2,1)S(1)}, u32[]{:S(2)}, u32[]{:S(2)}) collective-permute-start(bf16[3,128,128]{2,1,0:T(8,128)(2,1)S(1)} %bitcast.17), channel_id=1, source_target_pairs={{0,256},{256,0},{1,257},{257,1},{2,258},{258,2},{3,259},{259,3},{4... | collective-permute-start | bytes 294920 | tf_op jit(solution)/shard_map/ppermute | solution.py:346
  42.9 5.2 %copy-start.3 = (s32[1,96]{1,0:T(1,128)S(1)}, s32[1,96]{1,0:T(1,128)}, u32[]{:S(2)}) copy-start(s32[1,96]{1,0:T(1,128)} %param.10) | copy-start | bytes 1156
  42.9 5.9 %copy-start.4 = (s32[1,96]{1,0:T(1,128)S(1)}, s32[1,96]{1,0:T(1,128)}, u32[]{:S(2)}) copy-start(s32[1,96]{1,0:T(1,128)} %param.9) | copy-start | bytes 1156
  42.9 26.6 %all-to-all-start.1 = ((bf16[16,3,128,128]{3,2,1,0:T(8,128)(2,1)}), bf16[16,3,128,128]{3,2,1,0:T(8,128)(2,1)S(1)}, u32[]{:S(2)}, u32[]{:S(2)}) async-start(bf16[16,3,128,128]{3,2,1,0:T(8,128)(2,1)} %broadcast_in_dim.8), calls=%async_computation.1 | async-start | bytes 3145728 | tf_op jit(solution)/shard_map/all_to_all | solution.py:334
  73.0 6.4 %collective-permute-start.1 = (bf16[8,256,512]{2,1,0:T(8,128)(2,1)}, bf16[8,256,512]{2,1,0:T(8,128)(2,1)}, u32[]{:S(2)}, u32[]{:S(2)}) collective-permute-start(bf16[8,256,512]{2,1,0:T(8,128)(2,1)} %bitcast.13), channel_id=1, source_target_pairs={{0,1},{1,0},{2,3},{3,2},{4,5},{5,4},{6,7},{7,6},{8,9},{9,8},{10,11... | collective-permute-start | bytes 6291464 | tf_op jit(solution)/shard_map/ppermute | solution.py:372
  74.9 4.5 %copy-start = (bf16[2048,512]{1,0:T(8,128)(2,1)S(1)}, bf16[2048,512]{1,0:T(8,128)(2,1)}, u32[]{:S(2)}) copy-start(bf16[2048,512]{1,0:T(8,128)(2,1)} %all-gather.3.cloned.1.call-done) | copy-start | bytes 6291460
  74.9 4.5 %copy-start.1 = (f32[8192]{0:T(1024)S(1)}, f32[8192]{0:T(1024)}, u32[]{:S(2)}) copy-start(f32[8192]{0:T(1024)} %param.7) | copy-start | bytes 98308
  86.5 35.8 %collective-permute-start.2 = (bf16[8,128,128]{2,1,0:T(8,128)(2,1)S(1)}, bf16[8,128,128]{2,1,0:T(8,128)(2,1)S(1)}, u32[]{:S(2)}, u32[]{:S(2)}) collective-permute-start(bf16[8,128,128]{2,1,0:T(8,128)(2,1)S(1)} %get-tuple-element.30.k0_ref), channel_id=1, source_target_pairs={{0,256},{16,272},{32,288},{48,304},{64,320},{80,336},{96,352},{112... | collective-permute-start | bytes 786440 | tf_op jit(solution)/shard_map/ppermute | solution.py:376
  87.8 41.6 %collective-permute-start.6 = (bf16[8,128,128]{2,1,0:T(8,128)(2,1)S(1)}, bf16[8,128,128]{2,1,0:T(8,128)(2,1)S(1)}, u32[]{:S(2)}, u32[]{:S(2)}) collective-permute-start(bf16[8,128,128]{2,1,0:T(8,128)(2,1)S(1)} %get-tuple-element.30.k0_ref), channel_id=1, source_target_pairs={{0,64},{64,128},{128,192},{1,65},{65,129},{129,193},{2,66},{66,130... | collective-permute-start | bytes 786440 | tf_op jit(solution)/shard_map/ppermute | solution.py:379
  91.6 42.0 %all-to-all-start.2 = ((bf16[4,4,128,128]{3,2,1,0:T(8,128)(2,1)}), bf16[4,4,128,128]{3,2,1,0:T(8,128)(2,1)S(1)}, u32[]{:S(2)}, u32[]{:S(2)}) async-start(bf16[4,4,128,128]{3,2,1,0:T(8,128)(2,1)} %get-tuple-element.29), calls=%async_computation.2 | async-start | bytes 1048576 | tf_op jit(solution)/shard_map/all_to_all | solution.py:380
  95.9 37.7 %collective-permute-start.7 = (bf16[8,128,128]{2,1,0:T(8,128)(2,1)S(1)}, bf16[8,128,128]{2,1,0:T(8,128)(2,1)S(1)}, u32[]{:S(2)}, u32[]{:S(2)}) collective-permute-start(bf16[8,128,128]{2,1,0:T(8,128)(2,1)S(1)} %get-tuple-element.30.k0_ref), channel_id=1, source_target_pairs={{0,128},{64,192},{1,129},{65,193},{2,130},{66,194},{3,131},{67,195... | collective-permute-start | bytes 786440 | tf_op jit(solution)/shard_map/ppermute | solution.py:379
  100.5 33.1 %collective-permute-start.8 = (bf16[8,128,128]{2,1,0:T(8,128)(2,1)S(1)}, bf16[8,128,128]{2,1,0:T(8,128)(2,1)S(1)}, u32[]{:S(2)}, u32[]{:S(2)}) collective-permute-start(bf16[8,128,128]{2,1,0:T(8,128)(2,1)S(1)} %get-tuple-element.30.k0_ref), channel_id=1, source_target_pairs={{0,192},{1,193},{2,194},{3,195},{4,196},{5,197},{6,198},{7,199},{8... | collective-permute-start | bytes 786440 | tf_op jit(solution)/shard_map/ppermute | solution.py:379
  122.3 17.0 %collective-permute-start.5 = (bf16[8,128,128]{2,1,0:T(8,128)(2,1)S(1)}, bf16[8,128,128]{2,1,0:T(8,128)(2,1)S(1)}, u32[]{:S(2)}, u32[]{:S(2)}) collective-permute-start(bf16[8,128,128]{2,1,0:T(8,128)(2,1)S(1)} %collective-permute-done.2.k0_ref), channel_id=1, source_target_pairs={{256,320},{272,336},{288,352},{304,368},{320,384},{336,400},{352,4... | collective-permute-start | bytes 786440 | tf_op jit(solution)/shard_map/ppermute | solution.py:385
  126.1 16.6 %collective-permute-start.3 = (bf16[8,128,128]{2,1,0:T(8,128)(2,1)S(1)}, bf16[8,128,128]{2,1,0:T(8,128)(2,1)S(1)}, u32[]{:S(2)}, u32[]{:S(2)}) collective-permute-start(bf16[8,128,128]{2,1,0:T(8,128)(2,1)S(1)} %collective-permute-done.2.k0_ref), channel_id=1, source_target_pairs={{256,448},{272,464},{288,480},{304,496},{320,256},{336,272},{352,2... | collective-permute-start | bytes 786440 | tf_op jit(solution)/shard_map/ppermute | solution.py:385
  129.4 13.3 %collective-permute-start.4 = (bf16[8,128,128]{2,1,0:T(8,128)(2,1)S(1)}, bf16[8,128,128]{2,1,0:T(8,128)(2,1)S(1)}, u32[]{:S(2)}, u32[]{:S(2)}) collective-permute-start(bf16[8,128,128]{2,1,0:T(8,128)(2,1)S(1)} %collective-permute-done.2.k0_ref), channel_id=1, source_target_pairs={{256,384},{272,400},{288,416},{304,432},{320,448},{336,464},{352,4... | collective-permute-start | bytes 786440 | tf_op jit(solution)/shard_map/ppermute | solution.py:385
Sparse Core Ops, SparseCore 0:
  9.4 63.5 all-gather.2

commit v5 on v4

--- a/solution.py
+++ b/solution.py
@@ -67,11 +67,37 @@
     )(rows, cols, live, near_tiles, there_tiles)
 
 
-def project_kernel(core_ref, mine_ref, other_ref, w_ref, gain_ref, cos_ref, sin_ref,
-                   q_ref, kv_ref, acc_ref):
-    core = core_ref[0]
+def multiply(core, mine_ref, other_ref, w_ref, gain_ref, r, first, acc_ref):
     chunk = mine_ref.shape[2]
     per = chunk // HD
+    width = acc_ref.shape[1]
+    acc_ref[...] = jnp.zeros_like(acc_ref)
+
+    def step(i, c):
+        at = jnp.where(i < 4, 2 * i, 15 - 2 * i)
+        part = None
+        for ref, cc in ((mine_ref, core), (other_ref, 1 - core)):
+            x = ref[i].astype(jnp.float32) * r * gain_ref[2 * at + cc]
+            w = w_ref[pl.ds((2 * at + cc) * per, per), :, first:first + width]
+            d = jnp.dot(
+                x.astype(jnp.bfloat16),
+                w.reshape(chunk, width),
+                preferred_element_type=jnp.float32,
+            )
+            part = d if part is None else part + d
+        acc_ref[...] += part
+        return c
+
+    lax.fori_loop(0, 8, step, 0, unroll=8)
+
+
+def rot(v, cosines, sines):
+    return v * cosines + pltpu.roll(v, HD // 2, 1) * sines
+
+
+def keys_kernel(core_ref, mine_ref, other_ref, w_ref, gain_ref, cos_ref, sin_ref,
+                kv_ref, r_ref, acc_ref):
+    per = mine_ref.shape[2] // HD
 
     def square(i, tot):
         for ref in (mine_ref, other_ref):
@@ -82,53 +108,55 @@
 
     tot = lax.fori_loop(0, 8, square, jnp.zeros((TOK, HD), jnp.float32))
     r = lax.rsqrt(jnp.sum(tot, axis=1, keepdims=True) / D + 1e-05)
-    acc_ref[...] = jnp.zeros_like(acc_ref)
-
-    def step(i, c):
-        at = jnp.where(i < 4, 2 * i, 15 - 2 * i)
-        part = None
-        for ref, cc in ((mine_ref, core), (other_ref, 1 - core)):
-            x = ref[i].astype(jnp.float32) * r * gain_ref[2 * at + cc]
-            w = w_ref[pl.ds((2 * at + cc) * per, per)].reshape(chunk, COLS * HD)
-            d = jnp.dot(x.astype(jnp.bfloat16), w, preferred_element_type=jnp.float32)
-            part = d if part is None else part + d
-        acc_ref[...] += part
-        return c
-
-    lax.fori_loop(0, 8, step, 0, unroll=8)
-    cosines = cos_ref[...]
-    sines = sin_ref[...]
-
-    def rot(v):
-        return v * cosines + pltpu.roll(v, HD // 2, 1) * sines
-
+    r_ref[...] = jnp.broadcast_to(r, (TOK, HD))
+    multiply(core_ref[0], mine_ref, other_ref, w_ref, gain_ref, r, 2 * HD, acc_ref)
     for h in range(2):
-        q = rot(acc_ref[:, h * HD:(h + 1) * HD]) * SCALE
-        k = rot(acc_ref[:, (2 + h) * HD:(3 + h) * HD]).astype(jnp.bfloat16)
-        v = acc_ref[:, (4 + h) * HD:(5 + h) * HD]
+        k = rot(acc_ref[:, h * HD:(h + 1) * HD], cos_ref[...], sin_ref[...])
+        k = k.astype(jnp.bfloat16)
+        v = acc_ref[:, (2 + h) * HD:(3 + h) * HD]
         for half in range(2):
             at = slice(half * HD, (half + 1) * HD)
-            qt = q[at].T.astype(jnp.bfloat16)
+            kv_ref[4 * h + half] = k[at]
+            kv_ref[4 * h + 2 + half] = v[at].T.astype(jnp.bfloat16)
+
+
+def queries_kernel(core_ref, mine_ref, other_ref, w_ref, gain_ref, cos_ref, sin_ref, r_ref,
+                   q_ref, acc_ref):
+    r = r_ref[:, 0:1]
+    multiply(core_ref[0], mine_ref, other_ref, w_ref, gain_ref, r, 0, acc_ref)
+    for h in range(2):
+        q = rot(acc_ref[:, h * HD:(h + 1) * HD], cos_ref[...], sin_ref[...]) * SCALE
+        for half in range(2):
+            qt = q[half * HD:(half + 1) * HD].T.astype(jnp.bfloat16)
             for copy in range(4):
                 q_ref[copy, 2 * h + half] = qt
-            vt = v[at].T.astype(jnp.bfloat16)
-            kv_ref[4 * h + half] = k[at]
-            kv_ref[4 * h + 2 + half] = vt
-
-
-def project(core, mine, other, w, gain, cosines, sines):
-    return pl.pallas_call(
-        project_kernel,
+
+
+def project_keys(*args):
+    return pl.pallas_call(
+        keys_kernel,
         out_shape=(
-            jax.ShapeDtypeStruct((4, 4, HD, HD), jnp.bfloat16),
             jax.ShapeDtypeStruct((8, HD, HD), jnp.bfloat16),
+            jax.ShapeDtypeStruct((TOK, HD), jnp.float32),
         ),
         in_specs=[SM] + [VM] * 6,
         out_specs=(VM, VM),
-        scratch_shapes=[pltpu.VMEM((TOK, COLS * HD), jnp.float32)],
-        compiler_params=params(10),
-        name="project",
-    )(core, mine, other, w, gain, cosines, sines)
+        scratch_shapes=[pltpu.VMEM((TOK, 4 * HD), jnp.float32)],
+        compiler_params=params(10),
+        name="project_keys",
+    )(*args)
+
+
+def project_queries(*args):
+    return pl.pallas_call(
+        queries_kernel,
+        out_shape=jax.ShapeDtypeStruct((4, 4, HD, HD), jnp.bfloat16),
+        in_specs=[SM] + [VM] * 7,
+        out_specs=VM,
+        scratch_shapes=[pltpu.VMEM((TOK, 2 * HD), jnp.float32)],
+        compiler_params=params(10),
+        name="project_queries",
+    )(*args)
 
 
 SCALE = math.log2(math.e) / math.sqrt(HD)
@@ -371,12 +399,14 @@
     )
     other = lax.ppermute(mine, "core", [(0, 1), (1, 0)])
     w = scatter(rows, cols, live, near_tiles, there_tiles)
-    q, kv = project(core.reshape(1), mine, other, w, gain, cosines, sines)
+    parts = (core.reshape(1), mine, other, w, gain, cosines, sines)
+    kv, r = project_keys(*parts)
     across = [(b, 16 + b) for b in range(16)]
     fars = [lax.ppermute(kv, CTX, across)]
     keys = [kv]
     for k in range(1, 4):
         keys.append(lax.ppermute(kv, "y", [(y, y + k) for y in range(4 - k)]))
+    q = project_queries(*parts, r)
     q = lax.all_to_all(q, "x", 0, 0, tiled=True)
     for k in (1, 3, 2):
         pairs = [

time: 167 us -> 167 us (level)
  waiting for transfers between devices: 63.3 us -> 58.9 us
  local copies, waits for them, and re-layouts: 5.04 us -> 9.13 us
    unnamed x11 -> x19, local copies, waits for them, and re-layouts: 0.6 us -> 4.51 us
    ppermute x1, waiting for transfers between devices: 20.5 us -> 18.6 us  [body(): fars = [lax.ppermute(kv, CTX, across)]]
    pallas_call x1 -> x2, Pallas kernels: 7.12 us -> 6.11 us  [the longest x1 3.65 us: project_keys(): pl.pallas_call(keys_kernel, out_shape=(jax.ShapeDtypeStruct((8, HD, HD),...]
  transfers between devices with their start and end apart: 13 -> 13, of which waited for: 6 -> 5; matrix products, arithmetic and copies ran while one was open for 4% -> 4% of each run, Pallas kernels for 7% -> 9%
where the time goes in v5:
time: 167 us; the launch traced here: 166 us
  waiting for transfers between devices  58.9 us (35%)
  starting transfers between devices  45.5 us (27%)
  Pallas kernels  22.6 us (14%)
  between operations  14.3 us (9%)
  blocking collectives  13.5 us (8%)
  local copies, waits for them, and re-layouts  9.13 us (5%)
  other arithmetic  2.06 us (1%)
    all_to_all x2, waiting for transfers between devices, spread(): return lax.all_to_all(many, axis, 0, 0, tiled=True)  21.3 us
    ppermute x1, waiting for transfers between devices, body(): fars = [lax.ppermute(kv, CTX, across)]  18.6 us
    ppermute x1, waiting for transfers between devices, body(): there = lax.ppermute(tv, 'zh', [(0, 1), (1, 0)])  16.2 us
    all_to_all x1, blocking collectives, body(): return combine(lax.all_to_all(out, 'x', 0, 0, tiled=True))  13.5 us
    all_to_all x2, starting transfers between devices, spread(): return lax.all_to_all(many, axis, 0, 0, tiled=True)  11.7 us
    ppermute x3, starting transfers between devices, body(): fars.append(lax.ppermute(fars[0], CTX, pairs))  11.2 us
    ppermute x3, starting transfers between devices, body(): keys.append(lax.ppermute(kv, 'y', [(y, y + k) for y in range(4 - k)]))  9.75 us
    pallas_call x1, Pallas kernels, near(): pl.pallas_call(near_kernel, out_shape=STATE, in_specs=[SM] + [VM] * 5, ou...  5.67 us
  transfers between devices with their start and end apart: 13, of which 5 were waited for; matrix products, arithmetic and copies ran while one was open for 4% of the time, Pallas kernels for 9%

profile of v5, /device:TPU:448, one launch (start us, length us, event | category | flops | bytes accessed | tf_op | source)
XLA Modules:
  0.0 166.0 jit_solution(9223161054388910759)
XLA Ops:
  6.5 0.7 all-gather.3.cloned.1.call-update
  7.3 2.4 %broadcast_in_dim.7 = bf16[16,3,128,128]{3,2,1,0:T(8,128)(2,1)} broadcast(bf16[3,128,128]{2,1,0:T(8,128)(2,1)} %bitcast.18), dimensions={1,2,3} | broadcast | bytes 1671168 | tf_op jit(solution)/shard_map/broadcast_in_dim | solution.py:361
  9.7 7.2 %all-to-all-start = ((bf16[16,3,128,128]{3,2,1,0:T(8,128)(2,1)}), bf16[16,3,128,128]{3,2,1,0:T(8,128)(2,1)S(1)}, u32[]{:S(2)}, u32[]{:S(2)}) async-start(bf16[16,3,128,128]{3,2,1,0:T(8,128)(2,1)} %broadcast_in_dim.7), calls=%async_computation | async-start | bytes 3145728 | tf_op jit(solution)/shard_map/all_to_all | solution.py:362
  16.8 5.4 %collective-permute-start = (bf16[3,128,128]{2,1,0:T(8,128)(2,1)S(1)}, bf16[3,128,128]{2,1,0:T(8,128)(2,1)S(1)}, u32[]{:S(2)}, u32[]{:S(2)}) collective-permute-start(bf16[3,128,128]{2,1,0:T(8,128)(2,1)S(1)} %bitcast.19), channel_id=1, source_target_pairs={{0,256},{256,0},{1,257},{257,1},{2,258},{258,2},{3,259},{259,3},{4... | collective-permute-start | bytes 294920 | tf_op jit(solution)/shard_map/ppermute | solution.py:374
  22.3 16.2 %collective-permute-done = bf16[3,128,128]{2,1,0:T(8,128)(2,1)S(1)} collective-permute-done((bf16[3,128,128]{2,1,0:T(8,128)(2,1)S(1)}, bf16[3,128,128]{2,1,0:T(8,128)(2,1)S(1)}, u32[]{:S(2)}, u32[]{:S(2)}) %collective-permute-start) | collective-permute-done | bytes 98336 | tf_op jit(solution)/shard_map/ppermute | solution.py:374
  38.5 2.9 %all-to-all-done = bf16[16,3,128,128]{3,2,1,0:T(8,128)(2,1)S(1)} async-done(((bf16[16,3,128,128]{3,2,1,0:T(8,128)(2,1)}), bf16[16,3,128,128]{3,2,1,0:T(8,128)(2,1)S(1)}, u32[]{:S(2)}, u32[]{:S(2)}) %all-to-all-start) | async-done | bytes 1572896 | tf_op jit(solution)/shard_map/all_to_all | solution.py:362
  41.4 1.7 %broadcast_in_dim.8 = bf16[16,3,128,128]{3,2,1,0:T(8,128)(2,1)} broadcast(bf16[3,128,128]{2,1,0:T(8,128)(2,1)S(1)} %collective-permute-done), dimensions={1,2,3} | broadcast | bytes 1671168 | tf_op jit(solution)/shard_map/broadcast_in_dim | solution.py:361
  43.1 4.6 %all-to-all-start.1 = ((bf16[16,3,128,128]{3,2,1,0:T(8,128)(2,1)}), bf16[16,3,128,128]{3,2,1,0:T(8,128)(2,1)S(1)}, u32[]{:S(2)}, u32[]{:S(2)}) async-start(bf16[16,3,128,128]{3,2,1,0:T(8,128)(2,1)} %broadcast_in_dim.8), calls=%async_computation.1 | async-start | bytes 3145728 | tf_op jit(solution)/shard_map/all_to_all | solution.py:362
  48.9 0.6 reduce.6
  51.3 18.4 %all-to-all-done.1 = bf16[16,3,128,128]{3,2,1,0:T(8,128)(2,1)S(1)} async-done(((bf16[16,3,128,128]{3,2,1,0:T(8,128)(2,1)}), bf16[16,3,128,128]{3,2,1,0:T(8,128)(2,1)S(1)}, u32[]{:S(2)}, u32[]{:S(2)}) %all-to-all-start.1) | async-done | bytes 1572896 | tf_op jit(solution)/shard_map/all_to_all | solution.py:362
  69.7 1.2 copy-done.3
  70.9 2.1 %all-gather.3.cloned.1.call-done = bf16[2048,512]{1,0:T(8,128)(2,1)} async-done(((bf16[256,512]{1,0:T(8,128)(2,1)}), bf16[2048,512]{1,0:T(8,128)(2,1)}) %all-gather.3.cloned.1.call-update) | async-done | bytes 2097168 | tf_op jit(solution)/shard_map/all_gather | solution.py:370
  73.0 1.9 %collective-permute-start.1 = (bf16[8,256,512]{2,1,0:T(8,128)(2,1)}, bf16[8,256,512]{2,1,0:T(8,128)(2,1)S(1)}, u32[]{:S(2)}, u32[]{:S(2)}) collective-permute-start(bf16[8,256,512]{2,1,0:T(8,128)(2,1)} %bitcast.11), channel_id=1, source_target_pairs={{0,1},{1,0},{2,3},{3,2},{4,5},{5,4},{6,7},{7,6},{8,9},{9,8},{10,11... | collective-permute-start | bytes 6291464 | tf_op jit(solution)/shard_map/ppermute | solution.py:400
  74.9 1.4 copy-done.2
  76.3 1.4 copy-done.4
  77.7 3.1 %scatter_tiles.1.w_ref = bf16[64,128,768]{2,1,0:T(8,128)(2,1)S(1)} custom-call(s32[96]{0:T(128)S(1)} %reshape.48.row_ref, s32[96]{0:T(128)S(1)} %reshape.49.col_ref, s32[96]{0:T(128)S(1)} %reshape.54.live_ref, bf16[48,128,128]{2,1,0:T(8,128)(2,1)S(1)} %bitcast.14, bf16[48,128,128]{2,1,0:T(8,128)(2,1)S(1)} %bitcast.15), custom_call_target="tpu_custom_call" | custom-call | tf_op jit(solution)/shard_map/scatter_tiles/pallas_call | solution.py:60
  80.9 3.7 %project_keys.1 = (bf16[8,128,128]{2,1,0:T(8,128)(2,1)S(1)}, f32[256,128]{1,0:T(8,128)S(1)}) custom-call(s32[1]{0:T(128)} %bitcast.3.core_ref, bf16[8,256,512]{2,1,0:T(8,128)(2,1)S(1)} %bitcast.12, bf16[8,256,512]{2,1,0:T(8,128)(2,1)S(1)} %collective-permute-done.1.other_ref, bf16[64,128,768]{2,1,0:T(8,128)(2,1)S(1)} %scatter_tiles.1.w_ref, ...), custom_call_target="tpu_custom_call" | custom-call | tf_op jit(solution)/shard_map/project_keys/pallas_call | solution.py:136
  84.5 1.3 collective-permute-start.2
  85.8 3.9 %collective-permute-start.6 = (bf16[8,128,128]{2,1,0:T(8,128)(2,1)S(1)}, bf16[8,128,128]{2,1,0:T(8,128)(2,1)S(1)}, u32[]{:S(2)}, u32[]{:S(2)}) collective-permute-start(bf16[8,128,128]{2,1,0:T(8,128)(2,1)S(1)} %get-tuple-element.30.k0_ref), channel_id=1, source_target_pairs={{0,64},{64,128},{128,192},{1,65},{65,129},{129,193},{2,66},{66,130... | collective-permute-start | bytes 786440 | tf_op jit(solution)/shard_map/ppermute | solution.py:408
  89.7 2.5 %project_queries.1 = bf16[4,4,128,128]{3,2,1,0:T(8,128)(2,1)} custom-call(s32[1]{0:T(128)} %bitcast.3.core_ref, bf16[8,256,512]{2,1,0:T(8,128)(2,1)S(1)} %bitcast.13, bf16[8,256,512]{2,1,0:T(8,128)(2,1)S(1)} %collective-permute-done.1.other_ref, bf16[64,128,768]{2,1,0:T(8,128)(2,1)S(1)} %scatter_tiles.1.w_ref, f32[16,1,512]{2,1,0:T(1,128)S(1)} %bitcast.17, ...), custom_call_target="tpu_custom_call" | custom-call | tf_op jit(solution)/shard_map/project_queries/pallas_call | solution.py:151
  92.1 4.3 %all-to-all-start.2 = ((bf16[4,4,128,128]{3,2,1,0:T(8,128)(2,1)}), bf16[4,4,128,128]{3,2,1,0:T(8,128)(2,1)S(1)}, u32[]{:S(2)}, u32[]{:S(2)}) async-start(bf16[4,4,128,128]{3,2,1,0:T(8,128)(2,1)} %project_queries.1), calls=%async_computation.2 | async-start | bytes 1048576 | tf_op jit(solution)/shard_map/all_to_all | solution.py:410
  96.4 4.6 %collective-permute-start.7 = (bf16[8,128,128]{2,1,0:T(8,128)(2,1)S(1)}, bf16[8,128,128]{2,1,0:T(8,128)(2,1)S(1)}, u32[]{:S(2)}, u32[]{:S(2)}) collective-permute-start(bf16[8,128,128]{2,1,0:T(8,128)(2,1)S(1)} %get-tuple-element.30.k0_ref), channel_id=1, source_target_pairs={{0,128},{64,192},{1,129},{65,193},{2,130},{66,194},{3,131},{67,195... | collective-permute-start | bytes 786440 | tf_op jit(solution)/shard_map/ppermute | solution.py:408
  101.0 1.3 collective-permute-start.8
  102.3 18.6 %collective-permute-done.2.k0_ref = bf16[8,128,128]{2,1,0:T(8,128)(2,1)S(1)} collective-permute-done((bf16[8,128,128]{2,1,0:T(8,128)(2,1)S(1)}, bf16[8,128,128]{2,1,0:T(8,128)(2,1)S(1)}, u32[]{:S(2)}, u32[]{:S(2)}) %collective-permute-start.2) | collective-permute-done | bytes 262176 | tf_op jit(solution)/shard_map/ppermute | solution.py:405
  121.0 3.8 %collective-permute-start.5 = (bf16[8,128,128]{2,1,0:T(8,128)(2,1)S(1)}, bf16[8,128,128]{2,1,0:T(8,128)(2,1)S(1)}, u32[]{:S(2)}, u32[]{:S(2)}) collective-permute-start(bf16[8,128,128]{2,1,0:T(8,128)(2,1)S(1)} %collective-permute-done.2.k0_ref), channel_id=1, source_target_pairs={{256,320},{272,336},{288,352},{304,368},{320,384},{336,400},{352,4... | collective-permute-start | bytes 786440 | tf_op jit(solution)/shard_map/ppermute | solution.py:415
  124.8 3.2 %collective-permute-start.3 = (bf16[8,128,128]{2,1,0:T(8,128)(2,1)S(1)}, bf16[8,128,128]{2,1,0:T(8,128)(2,1)S(1)}, u32[]{:S(2)}, u32[]{:S(2)}) collective-permute-start(bf16[8,128,128]{2,1,0:T(8,128)(2,1)S(1)} %collective-permute-done.2.k0_ref), channel_id=1, source_target_pairs={{256,448},{272,464},{288,480},{304,496},{320,256},{336,272},{352,2... | collective-permute-start | bytes 786440 | tf_op jit(solution)/shard_map/ppermute | solution.py:415
  128.0 4.1 %collective-permute-start.4 = (bf16[8,128,128]{2,1,0:T(8,128)(2,1)S(1)}, bf16[8,128,128]{2,1,0:T(8,128)(2,1)S(1)}, u32[]{:S(2)}, u32[]{:S(2)}) collective-permute-start(bf16[8,128,128]{2,1,0:T(8,128)(2,1)S(1)} %collective-permute-done.2.k0_ref), channel_id=1, source_target_pairs={{256,384},{272,400},{288,416},{304,432},{320,448},{336,464},{352,4... | collective-permute-start | bytes 786440 | tf_op jit(solution)/shard_map/ppermute | solution.py:415
  132.3 5.7 %attend_near.1 = (f32[8,128,256]{2,1,0:T(8,128)S(1)}, f32[8,8,256]{2,1,0:T(8,128)S(1)}) custom-call(s32[3]{0:T(128)S(1)} %pad_add_fusion.ids_ref, bf16[4,4,128,128]{3,2,1,0:T(8,128)(2,1)S(1)} %all-to-all-done.2.q_ref, bf16[8,128,128]{2,1,0:T(8,128)(2,1)S(1)} %get-tuple-element.30.k0_ref, bf16[8,128,128]{2,1,0:T(8,128)(2,1)S(1)} %collective-permute-done.6.k1_ref, ...), custom_call_target="tpu_custom_call" | custom-call | tf_op jit(solution)/shard_map/attend_near/pallas_call | solution.py:220
  138.0 3.4 %attend_far.1 = (f32[8,128,256]{2,1,0:T(8,128)S(1)}, f32[8,8,256]{2,1,0:T(8,128)S(1)}) custom-call(s32[3]{0:T(128)S(1)} %pad_add_fusion.ids_ref, bf16[4,4,128,128]{3,2,1,0:T(8,128)(2,1)S(1)} %all-to-all-done.2.q_ref, bf16[8,128,128]{2,1,0:T(8,128)(2,1)S(1)} %collective-permute-done.2.k0_ref, bf16[8,128,128]{2,1,0:T(8,128)(2,1)S(1)} %collective-permute-done.5.k1_ref, ...), custom_call_target="tpu_custom_call" | custom-call | tf_op jit(solution)/shard_map/attend_far/pallas_call | solution.py:272
  141.4 3.5 %attend_last.1 = bf16[4,144,512]{2,1,0:T(8,128)(2,1)S(1)} custom-call(s32[3]{0:T(128)S(1)} %pad_add_fusion.ids_ref, bf16[4,4,128,128]{3,2,1,0:T(8,128)(2,1)S(1)} %all-to-all-done.2.q_ref, bf16[8,128,128]{2,1,0:T(8,128)(2,1)S(1)} %collective-permute-done.3.k0_ref, bf16[8,128,128]{2,1,0:T(8,128)(2,1)S(1)} %collective-permute-done.4.k1_ref, ...), custom_call_target="tpu_custom_call" | custom-call | tf_op jit(solution)/shard_map/attend_last/pallas_call | solution.py:322
  144.9 13.5 %all_to_all.20.parts_ref = bf16[4,144,512]{2,1,0:T(8,128)(2,1)S(1)} all-to-all(bf16[4,144,512]{2,1,0:T(8,128)(2,1)S(1)} %attend_last.1), channel_id=1, replica_groups=mesh['zh'=2,'y'=4,'x'=4,'zl'=8,'core'=2] {'x'}, dimensions={0} | all-to-all | bytes 1179648 | tf_op jit(solution)/shard_map/all_to_all | solution.py:420
  158.3 0.9 combine.1
  (42 shorter events, 2.5 us)
Async XLA Ops:
  6.5 66.4 %all-gather.3.cloned.1.call-start = ((), (), s32[]{:S(2)}) async-start(), calls=%async_computation.4 | async-start | bytes 2359296 | tf_op jit(solution)/shard_map/all_gather | solution.py:370
  9.7 7.2 %copy-start.6 = (bf16[1,3,128,128]{3,2,1,0:T(8,128)(2,1)S(1)}, bf16[1,3,128,128]{3,2,1,0:T(8,128)(2,1)}, u32[]{:S(2)}) copy-start(bf16[1,3,128,128]{3,2,1,0:T(8,128)(2,1)} %param.8) | copy-start | bytes 294916
  9.7 31.7 %all-to-all-start = ((bf16[16,3,128,128]{3,2,1,0:T(8,128)(2,1)}), bf16[16,3,128,128]{3,2,1,0:T(8,128)(2,1)S(1)}, u32[]{:S(2)}, u32[]{:S(2)}) async-start(bf16[16,3,128,128]{3,2,1,0:T(8,128)(2,1)} %broadcast_in_dim.7), calls=%async_computation | async-start | bytes 3145728 | tf_op jit(solution)/shard_map/all_to_all | solution.py:362
  16.8 21.6 %collective-permute-start = (bf16[3,128,128]{2,1,0:T(8,128)(2,1)S(1)}, bf16[3,128,128]{2,1,0:T(8,128)(2,1)S(1)}, u32[]{:S(2)}, u32[]{:S(2)}) collective-permute-start(bf16[3,128,128]{2,1,0:T(8,128)(2,1)S(1)} %bitcast.19), channel_id=1, source_target_pairs={{0,256},{256,0},{1,257},{257,1},{2,258},{258,2},{3,259},{259,3},{4... | collective-permute-start | bytes 294920 | tf_op jit(solution)/shard_map/ppermute | solution.py:374
  41.4 1.7 %copy-start.1 = (bf16[16,3,128,128]{3,2,1,0:T(8,128)(2,1)}, bf16[16,3,128,128]{3,2,1,0:T(8,128)(2,1)S(1)}, u32[]{:S(2)}) copy-start(bf16[16,3,128,128]{3,2,1,0:T(8,128)(2,1)S(1)} %all-to-all-done) | copy-start | bytes 4718596
  43.1 5.1 %copy-start.7 = (s32[1,96]{1,0:T(1,128)S(1)}, s32[1,96]{1,0:T(1,128)}, u32[]{:S(2)}) copy-start(s32[1,96]{1,0:T(1,128)} %param.10) | copy-start | bytes 1156
  43.1 5.9 %copy-start.8 = (s32[1,96]{1,0:T(1,128)S(1)}, s32[1,96]{1,0:T(1,128)}, u32[]{:S(2)}) copy-start(s32[1,96]{1,0:T(1,128)} %param.9) | copy-start | bytes 1156
  43.1 26.6 %all-to-all-start.1 = ((bf16[16,3,128,128]{3,2,1,0:T(8,128)(2,1)}), bf16[16,3,128,128]{3,2,1,0:T(8,128)(2,1)S(1)}, u32[]{:S(2)}, u32[]{:S(2)}) async-start(bf16[16,3,128,128]{3,2,1,0:T(8,128)(2,1)} %broadcast_in_dim.8), calls=%async_computation.1 | async-start | bytes 3145728 | tf_op jit(solution)/shard_map/all_to_all | solution.py:362
  69.7 1.2 copy-start.3
  73.0 7.9 %collective-permute-start.1 = (bf16[8,256,512]{2,1,0:T(8,128)(2,1)}, bf16[8,256,512]{2,1,0:T(8,128)(2,1)S(1)}, u32[]{:S(2)}, u32[]{:S(2)}) collective-permute-start(bf16[8,256,512]{2,1,0:T(8,128)(2,1)} %bitcast.11), channel_id=1, source_target_pairs={{0,1},{1,0},{2,3},{3,2},{4,5},{5,4},{6,7},{7,6},{8,9},{9,8},{10,11... | collective-permute-start | bytes 6291464 | tf_op jit(solution)/shard_map/ppermute | solution.py:400
  74.9 1.4 copy-start.2
  76.3 1.4 copy-start.4
  77.7 3.1 %copy-start = (bf16[2048,512]{1,0:T(8,128)(2,1)S(1)}, bf16[2048,512]{1,0:T(8,128)(2,1)}, u32[]{:S(2)}) copy-start(bf16[2048,512]{1,0:T(8,128)(2,1)} %all-gather.3.cloned.1.call-done) | copy-start | bytes 6291460
  77.7 3.1 %copy-start.5 = (f32[8192]{0:T(1024)S(1)}, f32[8192]{0:T(1024)}, u32[]{:S(2)}) copy-start(f32[8192]{0:T(1024)} %param.7) | copy-start | bytes 98308
  84.5 36.4 %collective-permute-start.2 = (bf16[8,128,128]{2,1,0:T(8,128)(2,1)S(1)}, bf16[8,128,128]{2,1,0:T(8,128)(2,1)S(1)}, u32[]{:S(2)}, u32[]{:S(2)}) collective-permute-start(bf16[8,128,128]{2,1,0:T(8,128)(2,1)S(1)} %get-tuple-element.30.k0_ref), channel_id=1, source_target_pairs={{0,256},{16,272},{32,288},{48,304},{64,320},{80,336},{96,352},{112... | collective-permute-start | bytes 786440 | tf_op jit(solution)/shard_map/ppermute | solution.py:405
  85.8 42.2 %collective-permute-start.6 = (bf16[8,128,128]{2,1,0:T(8,128)(2,1)S(1)}, bf16[8,128,128]{2,1,0:T(8,128)(2,1)S(1)}, u32[]{:S(2)}, u32[]{:S(2)}) collective-permute-start(bf16[8,128,128]{2,1,0:T(8,128)(2,1)S(1)} %get-tuple-element.30.k0_ref), channel_id=1, source_target_pairs={{0,64},{64,128},{128,192},{1,65},{65,129},{129,193},{2,66},{66,130... | collective-permute-start | bytes 786440 | tf_op jit(solution)/shard_map/ppermute | solution.py:408
  92.1 40.1 %all-to-all-start.2 = ((bf16[4,4,128,128]{3,2,1,0:T(8,128)(2,1)}), bf16[4,4,128,128]{3,2,1,0:T(8,128)(2,1)S(1)}, u32[]{:S(2)}, u32[]{:S(2)}) async-start(bf16[4,4,128,128]{3,2,1,0:T(8,128)(2,1)} %project_queries.1), calls=%async_computation.2 | async-start | bytes 1048576 | tf_op jit(solution)/shard_map/all_to_all | solution.py:410
  96.4 35.9 %collective-permute-start.7 = (bf16[8,128,128]{2,1,0:T(8,128)(2,1)S(1)}, bf16[8,128,128]{2,1,0:T(8,128)(2,1)S(1)}, u32[]{:S(2)}, u32[]{:S(2)}) collective-permute-start(bf16[8,128,128]{2,1,0:T(8,128)(2,1)S(1)} %get-tuple-element.30.k0_ref), channel_id=1, source_target_pairs={{0,128},{64,192},{1,129},{65,193},{2,130},{66,194},{3,131},{67,195... | collective-permute-start | bytes 786440 | tf_op jit(solution)/shard_map/ppermute | solution.py:408
  101.0 31.3 %collective-permute-start.8 = (bf16[8,128,128]{2,1,0:T(8,128)(2,1)S(1)}, bf16[8,128,128]{2,1,0:T(8,128)(2,1)S(1)}, u32[]{:S(2)}, u32[]{:S(2)}) collective-permute-start(bf16[8,128,128]{2,1,0:T(8,128)(2,1)S(1)} %get-tuple-element.30.k0_ref), channel_id=1, source_target_pairs={{0,192},{1,193},{2,194},{3,195},{4,196},{5,197},{6,198},{7,199},{8... | collective-permute-start | bytes 786440 | tf_op jit(solution)/shard_map/ppermute | solution.py:408
  121.0 17.0 %collective-permute-start.5 = (bf16[8,128,128]{2,1,0:T(8,128)(2,1)S(1)}, bf16[8,128,128]{2,1,0:T(8,128)(2,1)S(1)}, u32[]{:S(2)}, u32[]{:S(2)}) collective-permute-start(bf16[8,128,128]{2,1,0:T(8,128)(2,1)S(1)} %collective-permute-done.2.k0_ref), channel_id=1, source_target_pairs={{256,320},{272,336},{288,352},{304,368},{320,384},{336,400},{352,4... | collective-permute-start | bytes 786440 | tf_op jit(solution)/shard_map/ppermute | solution.py:415
  124.8 16.6 %collective-permute-start.3 = (bf16[8,128,128]{2,1,0:T(8,128)(2,1)S(1)}, bf16[8,128,128]{2,1,0:T(8,128)(2,1)S(1)}, u32[]{:S(2)}, u32[]{:S(2)}) collective-permute-start(bf16[8,128,128]{2,1,0:T(8,128)(2,1)S(1)} %collective-permute-done.2.k0_ref), channel_id=1, source_target_pairs={{256,448},{272,464},{288,480},{304,496},{320,256},{336,272},{352,2... | collective-permute-start | bytes 786440 | tf_op jit(solution)/shard_map/ppermute | solution.py:415
  128.0 13.4 %collective-permute-start.4 = (bf16[8,128,128]{2,1,0:T(8,128)(2,1)S(1)}, bf16[8,128,128]{2,1,0:T(8,128)(2,1)S(1)}, u32[]{:S(2)}, u32[]{:S(2)}) collective-permute-start(bf16[8,128,128]{2,1,0:T(8,128)(2,1)S(1)} %collective-permute-done.2.k0_ref), channel_id=1, source_target_pairs={{256,384},{272,400},{288,416},{304,432},{320,448},{336,464},{352,4... | collective-permute-start | bytes 786440 | tf_op jit(solution)/shard_map/ppermute | solution.py:415
Sparse Core Ops, SparseCore 0:
  9.4 63.5 all-gather.2
